TPU v7x, 32 devices: a whole 2x2x4 slice. The times are simulated.
32 devices in a mesh: groups: 2 (over y), ctx: 4 (over z), kv: 2 (over x), khalf: 2 (over core).
Axes of the slice: x: 2, y: 2, z: 4, core: 2. Of those that a mesh axis runs over, the one named last changes fastest.
Arguments:
- queries: bfloat16 [256, 8192], P(('groups', 'ctx'), 'kv'), parts along dimension 0, may hold values from -100 to 100
- cache_keys: bfloat16 [49152, 1024], P(('groups', 'ctx', 'khalf'), 'kv'), parts along dimension 0, may hold values from -7 to 7
- cache_values: bfloat16 [49152, 1024], P(('groups', 'ctx', 'khalf'), 'kv'), parts along dimension 0, may hold values from -6 to 6
- new_keys: bfloat16 [256, 1024], P(('groups', 'ctx'), 'kv'), parts along dimension 0, may hold values from -10 to 10
- new_values: bfloat16 [256, 1024], P(('groups', 'ctx'), 'kv'), parts along dimension 0, may hold values from -6 to 6
- cache_blocks: int32 [2], P('groups'), parts along dimension 0, may hold values from 48 to 192
- residual: bfloat16 [256, 8192], P('groups', ('ctx', 'khalf')), parts along dimension 0, may hold values from -20 to 20
- norm_gain: float32 [8192], P(('ctx', 'khalf')), may hold values from 0.1 to 1.9
- out_weight: bfloat16 [8192, 8192], P('kv', ('ctx', 'khalf')), may hold values from -0.0625 to 0.0625
- gate_up: bfloat16 [8192, 2, 14336], P(('ctx', 'khalf'), None, 'kv'), may hold values from -0.0625 to 0.0625
- down_weight: bfloat16 [14336, 8192], P('kv', ('ctx', 'khalf')), may hold values from -0.046875 to 0.046875
Outputs:
- layer_out: bfloat16 [256, 8192], P(('groups', 'kv'), ('ctx', 'khalf')), parts along dimension 0
There are 2 independent parts, one for each index of `groups`. A program takes and returns all parts, laid end to end along the dimension named above; an argument that names none is the same for every part. Nothing has to cross between parts.
Inputs may be any that keep to these rules, and one draw needn't show every extreme that they name: The first 128 * cache_blocks[0] cached positions are valid.
All inputs are finite; a program needn't handle non-finite values.
Results may differ from a plain program's by a relative error of at most 0.019.
Values may be sent and summed in bfloat16 or wider, within the bound.
No kernel may reach another device: no remote copies, remote signals or barrier semaphores. Data moves between devices by JAX's collectives and lax.ppermute only.
A program may use at most 128 MiB of HBM per device.

v0:
```python
import functools

import jax
import jax.numpy as jnp
from jax import lax
from jax.experimental import pallas as pl
from jax.experimental.pallas import tpu as pltpu
from jax.sharding import PartitionSpec as P


D = 8192
HQ = 64
KVH = 8
DH = 128
BLOCK = 128


NEG = -1e30
EPSILON = 1e-05
STREAMS = (4, 3)
SLABS = 2


def shifted(value, axis, by):
    devices = lax.axis_size(axis)
    return lax.ppermute(value, axis, [(i, (i + by) % devices) for i in range(devices)])


def merged_2(value, axis, combine):
    everything = jax.tree.map(
        lambda part, kind: lax.all_gather(part.astype(kind), axis),
        value,
        jax.tree.map(lambda a: jnp.bfloat16 if a.dtype == jnp.float32 else a.dtype, value),
    )

    def take(k):
        return jax.tree.map(lambda part, own: part[k].astype(own.dtype), everything, value)

    return lax.fori_loop(
        1, lax.axis_size(axis), lambda k, so_far: combine(so_far, take(k)), take(0)
    )


def attend(query_block, key_block, value_block, allowed):
    _, local_groups, _, head_width = query_block.shape
    key_count = key_block.shape[0]
    keyed = key_block.reshape(key_count, local_groups, head_width)
    valued = value_block.reshape(key_count, local_groups, head_width)
    scores = jnp.einsum(
        "rkgd,nkd->rkgn", query_block, keyed, preferred_element_type=jnp.float32
    ) * head_width ** (-0.5)
    usable = allowed[:, None, None, :]
    scores = jnp.where(usable, scores, NEG)
    peak_score = jnp.max(scores, axis=3)
    weights = jnp.where(usable, jnp.exp(scores - peak_score[..., None]), 0.0)
    weight_sum = jnp.sum(weights, axis=3)
    summed = jnp.einsum(
        "rkgn,nkd->rkgd", weights.astype(jnp.bfloat16), valued, preferred_element_type=jnp.float32
    )
    return (summed, peak_score, weight_sum)


def combine(earlier_part, later_part):
    earlier_sum, earlier_peak, earlier_total = earlier_part
    later_sum, later_peak, later_total = later_part
    new_peak = jnp.maximum(earlier_peak, later_peak)
    earlier_scale = jnp.exp(earlier_peak - new_peak)
    later_scale = jnp.exp(later_peak - new_peak)
    return (
        earlier_sum * earlier_scale[..., None] + later_sum * later_scale[..., None],
        new_peak,
        earlier_total * earlier_scale + later_total * later_scale,
    )


def normalize(hidden_state, norm_gain):
    values32 = hidden_state.astype(jnp.float32)
    squares = lax.psum(jnp.sum(values32 * values32, axis=1), ("ctx", "khalf"))
    factor = lax.rsqrt(squares / D + EPSILON)
    return (values32 * factor[:, None] * norm_gain).astype(jnp.bfloat16)


def on_device_any(
    queries,
    cache_keys,
    cache_values,
    new_keys,
    new_values,
    cache_blocks,
    residual,
    norm_gain,
    out_weight,
    gate_up,
    down_weight,
):
    query_rows = queries.shape[0]
    group_size = HQ // KVH
    local_groups = cache_keys.shape[1] // DH
    local_queries = queries.reshape(query_rows, local_groups, group_size, DH)
    cache_length = cache_keys.shape[0]
    shard_index = lax.axis_index("ctx") * lax.axis_size("khalf") + lax.axis_index("khalf")
    positions = shard_index * cache_length + jnp.arange(cache_length, dtype=jnp.int32)
    cache_allowed = (positions < cache_blocks[0] * BLOCK)[None, :]
    query_start = lax.axis_index("ctx") * query_rows
    query_positions = query_start + jnp.arange(query_rows, dtype=jnp.int32)
    empty = (
        jnp.zeros((query_rows, local_groups, group_size, DH), jnp.float32),
        jnp.full((query_rows, local_groups, group_size), NEG, jnp.float32),
        jnp.zeros((query_rows, local_groups, group_size), jnp.float32),
    )

    def cycle_step(step_index, state_carry):
        visiting, partial_state = state_carry
        fresh = attend(visiting, cache_keys, cache_values, cache_allowed)
        partial_state = combine(partial_state, fresh)
        visiting = shifted(visiting, "ctx", 1)
        partial_state = (
            shifted(partial_state[0].astype(jnp.bfloat16), "ctx", 1).astype(jnp.float32),
            shifted(partial_state[1].astype(jnp.bfloat16), "ctx", 1).astype(jnp.float32),
            shifted(partial_state[2].astype(jnp.bfloat16), "ctx", 1).astype(jnp.float32),
        )
        return (visiting, partial_state)

    _, cache_part = lax.fori_loop(0, lax.axis_size("ctx"), cycle_step, (local_queries, empty))
    merged = merged_2(cache_part, "khalf", combine)
    piece_keys = lax.all_gather(new_keys, "ctx", axis=0, tiled=True)
    piece_values = lax.all_gather(new_values, "ctx", axis=0, tiled=True)
    key_positions = jnp.arange(piece_keys.shape[0], dtype=jnp.int32)
    allowed = key_positions[None, :] <= query_positions[:, None]
    own_part = combine(empty, attend(local_queries, piece_keys, piece_values, allowed))
    joined = combine(merged, own_part)
    attention = (
        (joined[0] / joined[2][..., None])
        .astype(jnp.bfloat16)
        .reshape(query_rows, local_groups * group_size * DH)
    )
    partial_rows = jnp.dot(
        lax.all_gather(attention, "ctx", axis=0, tiled=True),
        out_weight,
        preferred_element_type=jnp.float32,
    )
    projected = lax.psum(partial_rows.astype(jnp.bfloat16), "kv").astype(jnp.float32)
    hidden_state = (residual.astype(jnp.float32) + projected).astype(jnp.bfloat16)
    normed = normalize(hidden_state, norm_gain)
    own_rows = hidden_state.shape[0] // lax.axis_size("kv")
    kept = lax.dynamic_slice_in_dim(hidden_state, lax.axis_index("kv") * own_rows, own_rows, 0)
    local_width = gate_up.shape[0]
    local_hidden = gate_up.shape[2]
    merged_weight = gate_up.reshape(local_width, 2 * local_hidden)
    both = lax.psum_scatter(
        jnp.dot(normed, merged_weight, preferred_element_type=jnp.float32).astype(jnp.bfloat16),
        ("ctx", "khalf"),
        scatter_dimension=0,
        tiled=True,
    ).astype(jnp.float32)
    activated = (jax.nn.silu(both[:, :local_hidden]) * both[:, local_hidden:]).astype(jnp.bfloat16)
    partial_out = jnp.dot(
        lax.all_gather(activated, ("ctx", "khalf"), axis=0, tiled=True),
        down_weight,
        preferred_element_type=jnp.float32,
    )
    down = lax.psum_scatter(
        partial_out.astype(jnp.bfloat16), "kv", scatter_dimension=0, tiled=True
    ).astype(jnp.float32)
    return (kept.astype(jnp.float32) + down).astype(jnp.bfloat16)


LOG2E = 1.4426950408889634
PIECES = 3
STAT_ROWS = 16
SMALL = 8 * 2**20
MEDIUM = 16 * 2**20
LARGE = 28 * 2**20
ALONE = 61 * 2**20
LOADING = 12 * 2**20
LANES = 4


def rotation(value, axis, by):
    devices = lax.axis_size(axis)
    return lax.ppermute(value, axis, [(i, (i + by) % devices) for i in range(devices)])


def exchanged(value, axis, bit):
    devices = lax.axis_size(axis)
    return lax.ppermute(value, axis, [(i, i ^ bit) for i in range(devices)])


def identity_mask(size):
    rows = lax.broadcasted_iota(jnp.int32, (size, size), 0)
    columns = lax.broadcasted_iota(jnp.int32, (size, size), 1)
    return rows == columns


def column_to_row(column, eye):
    return jnp.sum(jnp.where(eye, jnp.broadcast_to(column, eye.shape), 0.0), axis=0, keepdims=True)


def row_to_column(row, eye):
    return jnp.sum(jnp.where(eye, jnp.broadcast_to(row, eye.shape), 0.0), axis=1, keepdims=True)


def store_payload(ref, outs, lse_rows):
    count = len(outs)
    for at, block in enumerate(outs):
        ref[at * 128 : (at + 1) * 128, :] = block.astype(jnp.bfloat16)
    stats = jnp.concatenate(lse_rows, axis=0)
    high = stats.astype(jnp.bfloat16)
    rest = stats - high.astype(jnp.float32)
    middle = rest.astype(jnp.bfloat16)
    low = (rest - middle.astype(jnp.float32)).astype(jnp.bfloat16)
    pieces = [p.astype(jnp.float32) for p in (high, middle, low)]
    pad = jnp.zeros((STAT_ROWS - PIECES * count, 128), jnp.float32)
    ref[count * 128 : count * 128 + STAT_ROWS, :] = jnp.concatenate(pieces + [pad], axis=0).astype(
        jnp.bfloat16
    )


def attention_kernel(scal_ref, q_ref, nk_ref, nv_ref, *refs, sources, chunk, group_size, with_new):
    out_ref, q_buf, s_buf, max_buf, sum_buf, acc_buf, k_buf, v_buf, k_sems, v_sems = refs[
        2 * sources :
    ]
    rows_in = q_ref.shape[0]
    groups = q_ref.shape[1] // (group_size * DH)
    rows = rows_in * group_size
    length = refs[0].shape[0]
    steps = length // chunk
    factor = DH ** (-0.5) * LOG2E
    first = scal_ref[sources + 1]

    def columns(j):
        return pl.ds(pl.multiple_of((first + j) * DH, DH), DH)

    def copy_of(i, c, which):
        buffer, sems = ((k_buf, k_sems), (v_buf, v_sems))[which]
        return pltpu.make_async_copy(
            refs[2 * i + which].at[
                pl.ds(c * chunk, chunk), pl.ds(pl.multiple_of(first * DH, DH), groups * DH)
            ],
            buffer.at[pl.ds(i * length + c * chunk, chunk), :],
            sems.at[i * steps + c],
        )

    for which in (0, 1):
        for i in range(sources):
            for c in range(steps):

                @pl.when(c * chunk < scal_ref[i])
                def _(i=i, c=c, which=which):
                    copy_of(i, c, which).start()

    for j in range(groups):
        base = j * group_size * DH
        q_buf[j] = jnp.concatenate(
            [q_ref[:, base + h * DH : base + (h + 1) * DH] for h in range(group_size)], axis=0
        )
    max_buf[...] = jnp.full(max_buf.shape, NEG, jnp.float32)
    sum_buf[...] = jnp.zeros(sum_buf.shape, jnp.float32)
    acc_buf[...] = jnp.zeros(acc_buf.shape, jnp.float32)
    new_scores = []
    if with_new:
        shape = (rows, nk_ref.shape[0])
        new_masks = (
            lax.broadcasted_iota(jnp.int32, shape, 1)
            <= lax.broadcasted_iota(jnp.int32, shape, 0) % rows_in + scal_ref[sources]
        )
        for j in range(groups):
            fresh = lax.dot_general(
                q_buf[j],
                nk_ref[:, columns(j)],
                (((1,), (1,)), ((), ())),
                preferred_element_type=jnp.float32,
            )
            new_scores.append(jnp.where(new_masks, fresh, NEG))

    def wait_for(u, which):
        buffer, sems = ((k_buf, k_sems), (v_buf, v_sems))[which]
        pltpu.make_async_copy(
            refs[which].at[pl.ds(0, chunk), pl.ds(pl.multiple_of(first * DH, DH), groups * DH)],
            buffer.at[pl.ds(pl.multiple_of(u * chunk, chunk), chunk), :],
            sems.at[u],
        ).wait()

    def left_of(u):
        return scal_ref[u // steps] - u % steps * chunk

    def scores_of(u, left):
        span = pl.ds(pl.multiple_of(u * chunk, chunk), chunk)
        wait_for(u, 0)
        for j in range(groups):
            scores = lax.dot_general(
                q_buf[j],
                k_buf[span, j * DH : (j + 1) * DH],
                (((1,), (1,)), ((), ())),
                preferred_element_type=jnp.float32,
            )
            if left is not None:
                places = lax.broadcasted_iota(jnp.int32, scores.shape, 1)
                scores = jnp.where(places < left, scores, NEG)
            s_buf[j, :, span] = scores
            top = max_buf[j]
            for part in range(chunk // 128):
                top = jnp.maximum(top, scores[:, part * 128 : (part + 1) * 128])
            max_buf[j] = top

    def scores_step(u, carry):
        left = left_of(u)

        @pl.when(left >= chunk)
        def _():
            scores_of(u, None)

        @pl.when((left > 0) & (left < chunk))
        def _():
            scores_of(u, left)

        return carry

    lax.fori_loop(0, sources * steps, scores_step, 0)
    peaks = []
    for j in range(groups):
        peak = jnp.max(max_buf[j], axis=1, keepdims=True)
        if with_new:
            peak = jnp.maximum(peak, jnp.max(new_scores[j], axis=1, keepdims=True))
        peaks.append(peak * factor)

    def weights_step(u, carry):
        @pl.when(left_of(u) > 0)
        def _():
            span = pl.ds(pl.multiple_of(u * chunk, chunk), chunk)
            wait_for(u, 1)
            for j in range(groups):
                weights = jnp.exp2(s_buf[j, :, span] * factor - peaks[j])
                total = sum_buf[j]
                for part in range(chunk // 128):
                    total = total + weights[:, part * 128 : (part + 1) * 128]
                sum_buf[j] = total
                acc_buf[j] += jnp.dot(
                    weights.astype(jnp.bfloat16),
                    v_buf[span, j * DH : (j + 1) * DH],
                    preferred_element_type=jnp.float32,
                )

        return carry

    lax.fori_loop(0, sources * steps, weights_step, 0)
    eye = identity_mask(128)
    outs = []
    lse_rows = []
    for j in range(groups):
        total = jnp.sum(sum_buf[j], axis=1, keepdims=True)
        summed = acc_buf[j]
        if with_new:
            weights = jnp.where(new_masks, jnp.exp2(new_scores[j] * factor - peaks[j]), 0.0)
            total = total + jnp.sum(weights, axis=1, keepdims=True)
            summed = summed + jnp.dot(
                weights.astype(jnp.bfloat16),
                nv_ref[:, columns(j)],
                preferred_element_type=jnp.float32,
            )
        filled = total > 0.0
        safe = jnp.where(filled, total, 1.0)
        lse = jnp.where(filled, peaks[j] + jnp.log(safe) * LOG2E, NEG)
        result = summed / safe
        for part in range(rows // 128):
            span = slice(part * 128, (part + 1) * 128)
            outs.append(result[span])
            lse_rows.append(column_to_row(lse[span], eye))
    store_payload(out_ref, outs, lse_rows)


def merge_kernel(*refs, final, rows_in):
    parts, out_ref = refs[:-1], refs[-1]
    blocks = (parts[0].shape[0] - STAT_ROWS) // 128
    eye = identity_mask(128)
    lses = []
    for ref in parts:
        stats = ref[blocks * 128 : blocks * 128 + STAT_ROWS, :].astype(jnp.float32)
        lse = stats[0:blocks]
        for piece in range(1, PIECES):
            lse = lse + stats[piece * blocks : (piece + 1) * blocks]
        lses.append(lse)
    peak = lses[0]
    for lse in lses[1:]:
        peak = jnp.maximum(peak, lse)
    shares = [jnp.exp2(lse - peak) for lse in lses]
    total = shares[0]
    for share in shares[1:]:
        total = total + share
    outs = []
    for at in range(blocks):
        mixed = None
        for ref, share in zip(parts, shares):
            scale = row_to_column((share / total)[at : at + 1], eye)
            term = ref[at * 128 : (at + 1) * 128, :].astype(jnp.float32) * scale
            mixed = term if mixed is None else mixed + term
        outs.append(mixed)
    if not final:
        merged = peak + jnp.log(total) * LOG2E
        store_payload(out_ref, outs, [merged[at : at + 1] for at in range(blocks)])
        return
    heads_in = 128 // rows_in
    for at in range(blocks):
        for h in range(heads_in):
            head = at * heads_in + h
            out_ref[:, head * DH : (head + 1) * DH] = outs[at][
                h * rows_in : (h + 1) * rows_in
            ].astype(jnp.bfloat16)


def gather_rows(scal_ref, mine, other, left_buf):
    core = scal_ref[0]
    rows, half = mine[0].shape
    for s in range(len(mine)):
        at = pl.multiple_of(scal_ref[1 + s] * rows, rows)
        left_buf[pl.ds(at, rows), pl.ds(pl.multiple_of(core * half, half), half)] = mine[s][...]
        left_buf[pl.ds(at, rows), pl.ds(pl.multiple_of((1 - core) * half, half), half)] = other[s][
            ...
        ]


def projection_kernel(scal_ref, *refs, devices, start):
    mine, other = refs[:devices], refs[devices : 2 * devices]
    weight_ref, out_ref, left_buf = refs[2 * devices :]
    gather_rows(scal_ref, mine, other, left_buf)
    out_ref[...] = jnp.dot(
        left_buf[...],
        weight_ref[:, start : start + out_ref.shape[1]],
        preferred_element_type=jnp.float32,
    ).astype(jnp.bfloat16)


def prepare_kernel(scal_ref, residual_ref, gain_ref, *refs, parts):
    own, other = refs[:parts], refs[parts : 2 * parts]
    hidden_ref, left_ref, squares_ref = refs[2 * parts :]
    core = scal_ref[0]
    rows, width = residual_ref.shape
    half = rows // 2
    sums = [
        a[...].astype(jnp.float32) + b[...].astype(jnp.float32) for a, b in zip(own, other)
    ]
    values = residual_ref[...].astype(jnp.float32) + jnp.concatenate(sums, axis=1)
    hidden = values.astype(jnp.bfloat16)
    hidden_ref[...] = hidden
    values = hidden.astype(jnp.float32)
    squares = jnp.sum(values * values, axis=1, keepdims=True)
    squares_ref[...] = jnp.broadcast_to(column_to_row(squares, identity_mask(rows)), squares_ref.shape)
    gained = (values * gain_ref[...]).astype(jnp.bfloat16)
    low, high = gained[:half], gained[half:]
    keep = jnp.where(core == 0, low, high)
    send = jnp.where(core == 0, high, low)
    places = lax.broadcasted_iota(jnp.int32, (128, 256), 0) * 2
    spots = lax.broadcasted_iota(jnp.int32, (128, 256), 1)
    spread = [jnp.where(spots == places + s, 1.0, 0.0).astype(jnp.bfloat16) for s in (0, 1)]
    for k in range(width // 128):
        for at, source in ((0, keep), (2, send)):
            for s in (0, 1):
                left_ref[(at + s) * half : (at + s + 1) * half, k * 256 : (k + 1) * 256] = jnp.dot(
                    source[:, k * 128 : (k + 1) * 128], spread[s], preferred_element_type=jnp.float32
                ).astype(jnp.bfloat16)


def gate_up_kernel(left_ref, weight_ref, keep_ref, send_ref):
    rows = keep_ref.shape[0]
    depth, two, width = weight_ref.shape
    merged_weight = weight_ref.reshape(depth * two, width)[...]
    both = jnp.dot(left_ref[...], merged_weight, preferred_element_type=jnp.float32)
    keep_ref[...] = both[:rows].astype(jnp.bfloat16)
    send_ref[...] = both[rows:].astype(jnp.bfloat16)


def activation_kernel(scal_ref, own_ref, other_ref, squares_ref, out_ref):
    core = scal_ref[0]
    half = out_ref.shape[0]
    total = 2 * half
    both = own_ref[...].astype(jnp.float32) + other_ref[...].astype(jnp.float32)
    factor = lax.rsqrt(squares_ref[0:1, :] / D + EPSILON)
    column = row_to_column(factor, identity_mask(total))
    column = jnp.where(core == 0, column[:half], column[half:])
    gate = both[:half] * column
    up = both[half:] * column
    out_ref[...] = (gate / (1.0 + jnp.exp(-gate)) * up).astype(jnp.bfloat16)


def down_kernel(scal_ref, *refs, pieces, last):
    mine, other = refs[:pieces], refs[pieces : 2 * pieces]
    rest = refs[2 * pieces :]
    core = scal_ref[0]
    half, part = mine[0].shape
    if last:
        before_ref, weight_ref, keep_ref, send_ref, left_buf, out_buf = rest
    else:
        weight_ref, out_ref, left_buf = rest
    for s in range(pieces):
        span = pl.ds(pl.multiple_of(scal_ref[2 + s] * part, part), part)
        left_buf[pl.ds(pl.multiple_of(core * half, half), half), span] = mine[s][...]
        left_buf[pl.ds(pl.multiple_of((1 - core) * half, half), half), span] = other[s][...]
    product = jnp.dot(left_buf[...], weight_ref[...], preferred_element_type=jnp.float32)
    if not last:
        out_ref[...] = product
        return
    side = scal_ref[1]
    out_buf[...] = before_ref[...] + product
    keep_ref[...] = out_buf[pl.ds(pl.multiple_of(side * half, half), half), :]
    send_ref[...] = out_buf[pl.ds(pl.multiple_of((1 - side) * half, half), half), :].astype(
        jnp.bfloat16
    )


def load_kernel(source_ref, out_ref, sems, *, start):
    size = out_ref.shape[0] // LANES
    copies = [
        pltpu.make_async_copy(
            source_ref.at[pl.ds(start + i * size, size), :],
            out_ref.at[pl.ds(i * size, size), :],
            sems.at[i],
        )
        for i in range(LANES)
    ]
    for copy in copies:
        copy.start()
    for copy in copies:
        copy.wait()


def loaded(weight, start, count):
    return pl.pallas_call(
        functools.partial(load_kernel, start=start),
        out_shape=jax.ShapeDtypeStruct((count, weight.shape[1]), weight.dtype),
        in_specs=[far()],
        out_specs=vmem(),
        scratch_shapes=[pltpu.SemaphoreType.DMA((LANES,))],
        compiler_params=pltpu.CompilerParams(vmem_limit_bytes=LOADING),
        cost_estimate=cost(0, 4 * count * weight.shape[1]),
        name="load",
    )(weight)


def vmem():
    return pl.BlockSpec(memory_space=pltpu.VMEM)


def far():
    return pl.BlockSpec(memory_space=pltpu.HBM)


def smem():
    return pl.BlockSpec(memory_space=pltpu.SMEM)


def cost(flops, size):
    return pl.CostEstimate(flops=int(flops), bytes_accessed=int(size), transcendentals=0)


def attend_block(scal, with_new, queries, sources, new_keys, new_values, group_size):
    length, width = sources[0][0].shape
    rows_in = queries.shape[0]
    groups = width // DH // 2
    rows = rows_in * group_size
    chunk = next(c for c in (1536, 1024, 512, 256, 128) if length % c == 0)
    keys = len(sources) * length
    return pl.pallas_call(
        functools.partial(
            attention_kernel,
            sources=len(sources),
            chunk=chunk,
            group_size=group_size,
            with_new=with_new,
        ),
        out_shape=jax.ShapeDtypeStruct((groups * rows + STAT_ROWS, DH), jnp.bfloat16),
        in_specs=[smem()] + [vmem()] * 3 + [far()] * (2 * len(sources)),
        out_specs=vmem(),
        scratch_shapes=[
            pltpu.VMEM((groups, rows, DH), jnp.bfloat16),
            pltpu.VMEM((groups, rows, keys), jnp.float32),
            pltpu.VMEM((groups, rows, 128), jnp.float32),
            pltpu.VMEM((groups, rows, 128), jnp.float32),
            pltpu.VMEM((groups, rows, DH), jnp.float32),
            pltpu.VMEM((keys, groups * DH), jnp.bfloat16),
            pltpu.VMEM((keys, groups * DH), jnp.bfloat16),
            pltpu.SemaphoreType.DMA((keys // chunk,)),
            pltpu.SemaphoreType.DMA((keys // chunk,)),
        ],
        compiler_params=pltpu.CompilerParams(vmem_limit_bytes=ALONE if with_new and len(sources) == 1 else LARGE),
        cost_estimate=cost(4 * groups * rows * keys * DH * 3, 4 * keys * width),
        name="attend",
    )(scal, queries, new_keys, new_values, *[a for pair in sources for a in pair])


def merged(parts, final, rows_in):
    blocks = (parts[0].shape[0] - STAT_ROWS) // 128
    if final:
        shape = (rows_in, blocks * 128 // rows_in * DH)
    else:
        shape = parts[0].shape
    return pl.pallas_call(
        functools.partial(merge_kernel, final=final, rows_in=rows_in),
        out_shape=jax.ShapeDtypeStruct(shape, jnp.bfloat16),
        in_specs=[vmem()] * len(parts),
        out_specs=vmem(),
        cost_estimate=cost(blocks * 128 * 128 * 8 * len(parts), parts[0].size * 2 * len(parts)),
        compiler_params=pltpu.CompilerParams(vmem_limit_bytes=SMALL),
        name="merge",
    )(*parts)


def project(scal, mine, other, weight, start, count):
    devices = len(mine)
    rows = mine[0].shape[0] * devices
    depth = weight.shape[0]
    return pl.pallas_call(
        functools.partial(projection_kernel, devices=devices, start=start),
        out_shape=jax.ShapeDtypeStruct((rows, count), jnp.bfloat16),
        in_specs=[smem()] + [vmem()] * (2 * devices + 1),
        out_specs=vmem(),
        scratch_shapes=[pltpu.VMEM((rows, depth), jnp.bfloat16)],
        compiler_params=pltpu.CompilerParams(vmem_limit_bytes=MEDIUM),
        cost_estimate=cost(2 * rows * depth * count, 2 * depth * count),
        name="project",
    )(scal, *mine, *other, weight)


def prepare(scal, residual, gain, own, other):
    rows, width = residual.shape
    return pl.pallas_call(
        functools.partial(prepare_kernel, parts=len(own)),
        out_shape=(
            jax.ShapeDtypeStruct((rows, width), jnp.bfloat16),
            jax.ShapeDtypeStruct((2 * rows, 2 * width), jnp.bfloat16),
            jax.ShapeDtypeStruct((8, rows), jnp.float32),
        ),
        in_specs=[smem()] + [vmem()] * (2 + 2 * len(own)),
        out_specs=(vmem(),) * 3,
        cost_estimate=cost(rows * width * 1024, rows * width * 8),
        compiler_params=pltpu.CompilerParams(vmem_limit_bytes=SMALL),
        name="prepare",
    )(scal, residual, gain.reshape(1, width), *own, *other)


def gate_up_part(left, weight, start, count, tile):
    rows2, depth2 = left.shape
    depth = depth2 // 2
    rows = rows2 // 2
    first = start // tile
    out = jax.ShapeDtypeStruct((rows, count), jnp.bfloat16)
    return pl.pallas_call(
        gate_up_kernel,
        grid=(count // tile,),
        out_shape=(out, out),
        in_specs=[
            pl.BlockSpec((rows2, depth2), lambda i: (0, 0)),
            pl.BlockSpec((depth, 2, tile), lambda i: (0, 0, first + i)),
        ],
        out_specs=(
            pl.BlockSpec((rows, tile), lambda i: (0, i)),
            pl.BlockSpec((rows, tile), lambda i: (0, i)),
        ),
        compiler_params=pltpu.CompilerParams(vmem_limit_bytes=LARGE),
        cost_estimate=cost(2 * rows2 * depth2 * count, 4 * depth * count),
        name="gate_up",
    )(left, weight)


def activate(scal, own, other, squares):
    rows, width = own.shape
    return pl.pallas_call(
        activation_kernel,
        out_shape=jax.ShapeDtypeStruct((rows // 2, width), jnp.bfloat16),
        in_specs=[smem()] + [vmem()] * 3,
        out_specs=vmem(),
        cost_estimate=cost(rows * width * 16, rows * width * 5),
        compiler_params=pltpu.CompilerParams(vmem_limit_bytes=SMALL),
        name="activate",
    )(scal, own, other, squares)


def down_project(scal, mine, other, weight, before):
    pieces = len(mine)
    half, _ = mine[0].shape
    depth, width = weight.shape
    last = before is not None
    inputs = [*mine, *other] + ([before] if last else [])
    scratch = [pltpu.VMEM((2 * half, depth), jnp.bfloat16)]
    if last:
        out_shape = (
            jax.ShapeDtypeStruct((half, width), jnp.float32),
            jax.ShapeDtypeStruct((half, width), jnp.bfloat16),
        )
        out_specs = (vmem(), vmem())
        scratch.append(pltpu.VMEM((2 * half, width), jnp.float32))
    else:
        out_shape = jax.ShapeDtypeStruct((2 * half, width), jnp.float32)
        out_specs = vmem()
    return pl.pallas_call(
        functools.partial(down_kernel, pieces=pieces, last=last),
        in_specs=[smem()] + [vmem()] * (len(inputs) + 1),
        out_specs=out_specs,
        scratch_shapes=scratch,
        out_shape=out_shape,
        compiler_params=pltpu.CompilerParams(vmem_limit_bytes=MEDIUM),
        cost_estimate=cost(4 * half * depth * width, 2 * depth * width),
        name="down",
    )(scal, *inputs, weight)


def fold_kernel(scal_ref, own_ref, come_ref, away_ref, keep_ref):
    upper = scal_ref[0]
    width = keep_ref.shape[1]
    for out_ref, which in ((away_ref, 1 - upper), (keep_ref, upper)):
        span = pl.ds(pl.multiple_of(which * width, 128), width)
        out_ref[...] = (
            own_ref[:, span].astype(jnp.float32) + come_ref[:, span].astype(jnp.float32)
        ).astype(jnp.bfloat16)


def fold(scal, own, come):
    rows, width = own.shape
    out = jax.ShapeDtypeStruct((rows, width // 2), jnp.bfloat16)
    return pl.pallas_call(
        fold_kernel,
        out_shape=(out, out),
        in_specs=[smem()] + [vmem()] * 2,
        out_specs=(vmem(), vmem()),
        compiler_params=pltpu.CompilerParams(vmem_limit_bytes=SMALL),
        cost_estimate=cost(rows * width, rows * width * 6),
        name="fold",
    )(scal, own, come)


def half_of(value, which, axis=1):
    size = value.shape[axis] // 2
    return lax.dynamic_slice_in_dim(value, which * size, size, axis)


def on_device_line(
    queries,
    cache_keys,
    cache_values,
    new_keys,
    new_values,
    cache_blocks,
    residual,
    norm_gain,
    out_weight,
    gate_up,
    down_weight,
):
    devices = lax.axis_size("ctx")
    place = lax.axis_index("ctx")
    core = lax.axis_index("khalf")
    side = lax.axis_index("kv")
    group_size = HQ // KVH
    rows_in = queries.shape[0]
    length = cache_keys.shape[0]
    mine_valid, other_valid = (
        jnp.clip(cache_blocks[0] * BLOCK - (place * 2 + c) * length, 0, length)
        for c in (core, 1 - core)
    )
    bits = [1 << b for b in range(devices.bit_length() - 1)]
    sources = [(place - s) % devices for s in range(devices)]
    blocks = [
        sum((source // bit) % 2 * (devices // (2 * bit)) for bit in bits) for source in sources
    ]
    groups = cache_keys.shape[1] // DH // 2
    offsets = [(source - place) * rows_in for source in sources]

    def packed(*values):
        return jnp.stack(values).astype(jnp.int32)

    early = (
        half_of(queries, core),
        packed(mine_valid, 0, core * groups),
        packed(other_valid, 0, core * groups),
        [packed(mine_valid, other_valid, o, core * groups) for o in offsets[1:]],
        packed(core, *sources),
        packed(core, side),
        packed(core, side, *blocks),
        [packed((place // bit) % 2) for bit in bits],
    )
    early = lax.optimization_barrier(early)
    q_mine, own_scal, rest_scal, visit_scals, source_scal, core_scal, down_scal, bit_scals = early
    order = sorted(range(1, devices), key=lambda s: min(s, devices - s))
    visiting = {}
    for s in order:
        visiting[s] = rotation(q_mine, "ctx", s)
    k_there = exchanged(cache_keys, "khalf", 1)
    v_there = exchanged(cache_values, "khalf", 1)
    here, there = (cache_keys, cache_values), (k_there, v_there)
    last = attend_block(
        own_scal, True, q_mine, [here], new_keys, new_values, group_size
    )
    parts = [last]
    for s in order:
        visitor, last = lax.optimization_barrier((visiting[s], last))
        last = attend_block(
            visit_scals[s - 1],
            True,
            visitor,
            [here, there],
            new_keys,
            new_values,
            group_size,
        )
        parts.append(rotation(last, "ctx", -s))
    q_mine, last = lax.optimization_barrier((q_mine, last))
    parts.append(attend_block(rest_scal, False, q_mine, [there], new_keys, new_values, group_size))
    attention = merged(parts, True, rows_in)
    mine = [attention]
    for s in range(1, devices):
        mine.append(rotation(attention, "ctx", s))
    other = [exchanged(a, "khalf", 1) for a in mine]
    out_near = loaded(out_weight, 0, out_weight.shape[0])
    own, come = [], []
    width = out_weight.shape[1] // SLABS
    for slab in range(SLABS):
        own.append(project(source_scal, mine, other, out_near, slab * width, width))
        come.append(exchanged(own[-1], "kv", 1))
    hidden, left, squares = prepare(core_scal, residual, norm_gain, own, come)
    for bit in bits:
        squares = squares + exchanged(squares, "ctx", bit)
    squares = squares + exchanged(squares, "khalf", 1)
    unit = gate_up.shape[2] // sum(STREAMS)
    starts = [unit * sum(STREAMS[:i]) for i in range(len(STREAMS))]
    spans = [unit * share for share in STREAMS]
    down = None
    down_near = []
    for start, span in zip(starts, spans):
        down_near.append(loaded(down_weight, start, span))
    for stream, (start, span) in enumerate(zip(starts, spans)):
        keep, send = gate_up_part(left, gate_up, start, span, unit)
        come = exchanged(send, "khalf", 1)
        for bit, bit_scal in zip(bits, bit_scals):
            away, keep = fold(bit_scal, keep, come)
            if bit == 1:
                away, left = lax.optimization_barrier((away, left))
            come = exchanged(away, "ctx", bit)
        activated = activate(core_scal, keep, come, squares)
        mine, other = [], []
        for s in range(devices):
            piece = activated
            if s:
                piece = rotation(activated, "ctx", s)
            mine.append(piece)
            other.append(exchanged(piece, "khalf", 1))
        down = down_project(down_scal, mine, other, down_near[stream], down)
    keep, send = down
    come = exchanged(send, "kv", 1)
    kept = half_of(hidden, side, 0)
    return (kept.astype(jnp.float32) + keep + come.astype(jnp.float32)).astype(jnp.bfloat16)


def line_fits(mesh, keys_shape, hidden_width):
    sizes = dict(mesh.shape)
    ctx, kv, khalf = sizes["ctx"], sizes["kv"], sizes["khalf"]
    groups = keys_shape[1] // kv // DH
    length = keys_shape[0] // (sizes["groups"] * ctx * khalf)
    return (
        ctx & (ctx - 1) == 0
        and kv == 2
        and khalf == 2
        and groups % 2 == 0
        and length % 128 == 0
        and hidden_width // kv % (sum(STREAMS) * ctx * 128) == 0
    )


def solution(mesh):
    def on_device(*arguments):
        keys, gate_up = arguments[1], arguments[9]
        sizes = dict(mesh.shape)
        keys_shape = (
            keys.shape[0] * sizes["groups"] * sizes["ctx"] * sizes["khalf"],
            keys.shape[1] * sizes["kv"],
        )
        if line_fits(mesh, keys_shape, gate_up.shape[2] * sizes["kv"]):
            return on_device_line(*arguments)
        return on_device_any(*arguments)

    in_specs = (
        P(("groups", "ctx"), "kv"),
        P(("groups", "ctx", "khalf"), "kv"),
        P(("groups", "ctx", "khalf"), "kv"),
        P(("groups", "ctx"), "kv"),
        P(("groups", "ctx"), "kv"),
        P("groups"),
        P("groups", ("ctx", "khalf")),
        P(("ctx", "khalf")),
        P("kv", ("ctx", "khalf")),
        P(("ctx", "khalf"), None, "kv"),
        P("kv", ("ctx", "khalf")),
    )
    out_specs = P(("groups", "kv"), ("ctx", "khalf"))
    return jax.shard_map(
        on_device, mesh=mesh, in_specs=in_specs, out_specs=out_specs, check_vma=False
    )
```

profile of v0, /device:TPU:0, one launch (start us, length us, event | category | flops | bytes accessed | tf_op | source)
XLA Modules:
  0.0 172.6 jit_solution(14523061469106900016)
XLA Ops:
  2.4 3.0 %collective-permute-start = (bf16[32,2048]{1,0:T(8,128)(2,1)S(1)}, bf16[32,2048]{1,0:T(8,128)(2,1)S(1)}, u32[]{:S(2)}, u32[]{:S(2)}) collective-permute-start(bf16[32,2048]{1,0:T(8,128)(2,1)S(1)} %constant_dynamic-slice_fusion.q_ref), channel_id=1, source_target_pairs={{0,4},{4,8},{8,12},{12,0},{1,5},{5,9},{9,13},{13,1},{2,6},{6,10},{... | collective-permute-start | bytes 393224 | tf_op jit(solution)/shard_map/ppermute | solution.py:181
  5.4 2.1 %collective-permute-start.4 = (bf16[32,2048]{1,0:T(8,128)(2,1)S(1)}, bf16[32,2048]{1,0:T(8,128)(2,1)S(1)}, u32[]{:S(2)}, u32[]{:S(2)}) collective-permute-start(bf16[32,2048]{1,0:T(8,128)(2,1)S(1)} %constant_dynamic-slice_fusion.q_ref), channel_id=1, source_target_pairs={{0,12},{4,0},{8,4},{12,8},{1,13},{5,1},{9,5},{13,9},{2,14},{6,2},{... | collective-permute-start | bytes 393224 | tf_op jit(solution)/shard_map/ppermute | solution.py:181
  7.5 0.9 collective-permute-start.6
  8.5 5.9 %attend.5.refs_0_ = bf16[528,128]{1,0:T(8,128)(2,1)} custom-call(s32[3]{0:T(128)} %get-tuple-element.42.scal_ref, bf16[32,2048]{1,0:T(8,128)(2,1)} %copy-done.4, bf16[32,512]{1,0:T(8,128)(2,1)} %nk_ref.9, bf16[32,512]{1,0:T(8,128)(2,1)} %nv_ref.9, bf16[3072,512]{1,0:T(8,128)(2,1)} %refs_0_.7, bf16[3072,512]{1,0:T(8,128)(2,1)} %refs_1_.7), custom_call_target="tpu_custom_call" | custom-call | flops 2415919104 | bytes 6291456 | tf_op jit(solution)/shard_map/attend/pallas_call | solution.py:562
  14.4 1.9 %copy-done.7 = bf16[3072,512]{1,0:T(8,128)(2,1)S(1)} copy-done((bf16[3072,512]{1,0:T(8,128)(2,1)S(1)}, bf16[3072,512]{1,0:T(8,128)(2,1)}, u32[]{:S(2)}) %copy-start.7) | copy-done | bytes 3145752
  16.3 1.9 %copy-done.8 = bf16[3072,512]{1,0:T(8,128)(2,1)S(1)} copy-done((bf16[3072,512]{1,0:T(8,128)(2,1)S(1)}, bf16[3072,512]{1,0:T(8,128)(2,1)}, u32[]{:S(2)}) %copy-start.8) | copy-done | bytes 3145752
  18.2 6.8 %attend.6 = bf16[528,128]{1,0:T(8,128)(2,1)S(1)} custom-call(s32[4]{0:T(128)S(1)} %get-tuple-element.44.scal_ref, bf16[32,2048]{1,0:T(8,128)(2,1)S(1)} %collective-permute-done.q_ref, bf16[32,512]{1,0:T(8,128)(2,1)S(1)} %copy-done.9, bf16[32,512]{1,0:T(8,128)(2,1)S(1)} %copy-done.10, bf16[3072,512]{1,0:T(8,128)(2,1)S(1)} %copy-done.7, ...), custom_call_target="tpu_custom_call" | custom-call | flops 4831838208 | bytes 12582912 | tf_op jit(solution)/shard_map/attend/pallas_call | solution.py:562
  25.1 6.8 %attend.7 = bf16[528,128]{1,0:T(8,128)(2,1)S(1)} custom-call(s32[4]{0:T(128)S(1)} %add_add_fusion.2.scal_ref, bf16[32,2048]{1,0:T(8,128)(2,1)S(1)} %collective-permute-done.4.q_ref, bf16[32,512]{1,0:T(8,128)(2,1)S(1)} %copy-done.9, bf16[32,512]{1,0:T(8,128)(2,1)S(1)} %copy-done.10, bf16[3072,512]{1,0:T(8,128)(2,1)S(1)} %copy-done.7, ...), custom_call_target="tpu_custom_call" | custom-call | flops 4831838208 | bytes 12582912 | tf_op jit(solution)/shard_map/attend/pallas_call | solution.py:562
  31.9 2.0 %collective-permute-start.5 = (bf16[528,128]{1,0:T(8,128)(2,1)S(1)}, bf16[528,128]{1,0:T(8,128)(2,1)S(1)}, u32[]{:S(2)}, u32[]{:S(2)}) collective-permute-start(bf16[528,128]{1,0:T(8,128)(2,1)S(1)} %attend.7), channel_id=1, source_target_pairs={{0,4},{4,8},{8,12},{12,0},{1,5},{5,9},{9,13},{13,1},{2,6},{6,10},{... | collective-permute-start | bytes 405512 | tf_op jit(solution)/shard_map/ppermute | solution.py:181
  34.0 7.0 %attend.8 = bf16[528,128]{1,0:T(8,128)(2,1)S(1)} custom-call(s32[4]{0:T(128)S(1)} %get-tuple-element.48.scal_ref, bf16[32,2048]{1,0:T(8,128)(2,1)S(1)} %collective-permute-done.6.q_ref, bf16[32,512]{1,0:T(8,128)(2,1)S(1)} %copy-done.9, bf16[32,512]{1,0:T(8,128)(2,1)S(1)} %copy-done.10, bf16[3072,512]{1,0:T(8,128)(2,1)S(1)} %copy-done.7, ...), custom_call_target="tpu_custom_call" | custom-call | flops 4831838208 | bytes 12582912 | tf_op jit(solution)/shard_map/attend/pallas_call | solution.py:562
  41.1 4.9 %attend.9.refs_4_ = bf16[528,128]{1,0:T(8,128)(2,1)S(1)} custom-call(s32[3]{0:T(128)S(1)} %get-tuple-element.50.scal_ref, bf16[32,2048]{1,0:T(8,128)(2,1)S(1)} %copy-done.5, bf16[32,512]{1,0:T(8,128)(2,1)S(1)} %copy-done.9, bf16[32,512]{1,0:T(8,128)(2,1)S(1)} %copy-done.10, bf16[3072,512]{1,0:T(8,128)(2,1)} %collective-permute-done.1.refs_2_.refs_0_, ...), custom_call_target="tpu_custom_call" | custom-call | flops 2415919104 | bytes 6291456 | tf_op jit(solution)/shard_map/attend/pallas_call | solution.py:562
  46.0 2.8 %collective-permute-done.7.refs_3_ = bf16[528,128]{1,0:T(8,128)(2,1)S(1)} collective-permute-done((bf16[528,128]{1,0:T(8,128)(2,1)S(1)}, bf16[528,128]{1,0:T(8,128)(2,1)S(1)}, u32[]{:S(2)}, u32[]{:S(2)}) %collective-permute-start.7) | collective-permute-done | bytes 135200 | tf_op jit(solution)/shard_map/ppermute | solution.py:181
  49.2 0.8 collective-permute-start.9
  50.1 3.0 %collective-permute-start.10 = (bf16[32,2048]{1,0:T(8,128)(2,1)S(1)}, bf16[32,2048]{1,0:T(8,128)(2,1)S(1)}, u32[]{:S(2)}, u32[]{:S(2)}) collective-permute-start(bf16[32,2048]{1,0:T(8,128)(2,1)S(1)} %merge.1.refs_0_), channel_id=1, source_target_pairs={{0,12},{4,0},{8,4},{12,8},{1,13},{5,1},{9,5},{13,9},{2,14},{6,2},{... | collective-permute-start | bytes 393224 | tf_op jit(solution)/shard_map/ppermute | solution.py:181
  53.1 4.3 %collective-permute-done.8.refs_1_ = bf16[32,2048]{1,0:T(8,128)(2,1)S(1)} collective-permute-done((bf16[32,2048]{1,0:T(8,128)(2,1)S(1)}, bf16[32,2048]{1,0:T(8,128)(2,1)S(1)}, u32[]{:S(2)}, u32[]{:S(2)}) %collective-permute-start.8) | collective-permute-done | bytes 131104 | tf_op jit(solution)/shard_map/ppermute | solution.py:181
  57.4 4.2 %collective-permute-done.9.refs_2_ = bf16[32,2048]{1,0:T(8,128)(2,1)S(1)} collective-permute-done((bf16[32,2048]{1,0:T(8,128)(2,1)S(1)}, bf16[32,2048]{1,0:T(8,128)(2,1)S(1)}, u32[]{:S(2)}, u32[]{:S(2)}) %collective-permute-start.9) | collective-permute-done | bytes 131104 | tf_op jit(solution)/shard_map/ppermute | solution.py:181
  63.1 1.3 project.2.refs_0_
  64.5 1.6 collective-permute-start.15
  66.0 1.3 project.3.refs_1_
  67.9 2.5 %collective-permute-done.15.refs_2_ = bf16[128,512]{1,0:T(8,128)(2,1)S(1)} collective-permute-done((bf16[128,512]{1,0:T(8,128)(2,1)S(1)}, bf16[128,512]{1,0:T(8,128)(2,1)S(1)}, u32[]{:S(2)}, u32[]{:S(2)}) %collective-permute-start.15) | collective-permute-done | bytes 131104 | tf_op jit(solution)/shard_map/ppermute | solution.py:186
  70.5 2.6 %collective-permute-done.16.refs_3_ = bf16[128,512]{1,0:T(8,128)(2,1)S(1)} collective-permute-done((bf16[128,512]{1,0:T(8,128)(2,1)S(1)}, bf16[128,512]{1,0:T(8,128)(2,1)S(1)}, u32[]{:S(2)}, u32[]{:S(2)}) %collective-permute-start.16) | collective-permute-done | bytes 131104 | tf_op jit(solution)/shard_map/ppermute | solution.py:186
  73.1 1.0 prepare.1
  74.1 8.5 %gate_up.2 = (bf16[128,4096]{1,0:T(8,128)(2,1)S(1)}, bf16[128,4096]{1,0:T(8,128)(2,1)S(1)}) custom-call(bf16[256,2048]{1,0:T(8,128)(2,1)S(1)} %get-tuple-element.60.left_ref, bf16[1024,2,7168]{2,1,0:T(2,128)(2,1)} %weight_ref.3), custom_call_target="tpu_custom_call" | custom-call | flops 4294967296 | bytes 16777216 | tf_op jit(solution)/shard_map/gate_up/pallas_call | solution.py:646
  82.7 2.6 %collective-permute-done.17.come_ref = bf16[128,4096]{1,0:T(8,128)(2,1)S(1)} collective-permute-done((bf16[128,4096]{1,0:T(8,128)(2,1)S(1)}, bf16[128,4096]{1,0:T(8,128)(2,1)S(1)}, u32[]{:S(2)}, u32[]{:S(2)}) %collective-permute-start.17) | collective-permute-done | bytes 1048608 | tf_op jit(solution)/shard_map/ppermute | solution.py:186
  85.7 8.0 %gate_up.3 = (bf16[128,3072]{1,0:T(8,128)(2,1)S(1)}, bf16[128,3072]{1,0:T(8,128)(2,1)S(1)}) custom-call(bf16[256,2048]{1,0:T(8,128)(2,1)S(1)} %get-tuple-element.60.left_ref, bf16[1024,2,7168]{2,1,0:T(2,128)(2,1)} %weight_ref.3), custom_call_target="tpu_custom_call" | custom-call | flops 3221225472 | bytes 12582912 | tf_op jit(solution)/shard_map/gate_up/pallas_call | solution.py:646
  93.8 2.1 %collective-permute-start.31 = (bf16[128,2048]{1,0:T(8,128)(2,1)S(1)}, bf16[128,2048]{1,0:T(8,128)(2,1)S(1)}, u32[]{:S(2)}, u32[]{:S(2)}) collective-permute-start(bf16[128,2048]{1,0:T(8,128)(2,1)S(1)} %get-tuple-element.70), channel_id=1, source_target_pairs={{0,4},{4,0},{8,12},{12,8},{1,5},{5,1},{9,13},{13,9},{2,6},{6,2},{1... | collective-permute-start | bytes 1572872 | tf_op jit(solution)/shard_map/ppermute | solution.py:186
  96.2 2.1 %collective-permute-start.19 = (bf16[128,1536]{1,0:T(8,128)(2,1)S(1)}, bf16[128,1536]{1,0:T(8,128)(2,1)S(1)}, u32[]{:S(2)}, u32[]{:S(2)}) collective-permute-start(bf16[128,1536]{1,0:T(8,128)(2,1)S(1)} %get-tuple-element.65), channel_id=1, source_target_pairs={{0,4},{4,0},{8,12},{12,8},{1,5},{5,1},{9,13},{13,9},{2,6},{6,2},{1... | collective-permute-start | bytes 1179656 | tf_op jit(solution)/shard_map/ppermute | solution.py:186
  98.3 10.4 %collective-permute-done.31.come_ref = bf16[128,2048]{1,0:T(8,128)(2,1)S(1)} collective-permute-done((bf16[128,2048]{1,0:T(8,128)(2,1)S(1)}, bf16[128,2048]{1,0:T(8,128)(2,1)S(1)}, u32[]{:S(2)}, u32[]{:S(2)}) %collective-permute-start.31) | collective-permute-done | bytes 524320 | tf_op jit(solution)/shard_map/ppermute | solution.py:186
  108.8 1.1 collective-permute-start.32
  109.9 1.7 collective-permute-start.21
  111.6 10.5 %collective-permute-done.21 = f32[8,128]{1,0:T(8,128)S(1)} collective-permute-done((f32[8,128]{1,0:T(8,128)S(1)}, f32[8,128]{1,0:T(8,128)S(1)}, u32[]{:S(2)}, u32[]{:S(2)}) %collective-permute-start.21) | collective-permute-done | bytes 4128 | tf_op jit(solution)/shard_map/ppermute | solution.py:186
  122.1 1.2 collective-permute-start.22
  123.3 3.3 %collective-permute-done.22 = f32[8,128]{1,0:T(8,128)S(1)} collective-permute-done((f32[8,128]{1,0:T(8,128)S(1)}, f32[8,128]{1,0:T(8,128)S(1)}, u32[]{:S(2)}, u32[]{:S(2)}) %collective-permute-start.22) | collective-permute-done | bytes 4128 | tf_op jit(solution)/shard_map/ppermute | solution.py:186
  126.6 1.2 collective-permute-done.23
  127.8 0.7 activate.3.refs_0_
  128.5 2.2 %collective-permute-start.33 = (bf16[64,1024]{1,0:T(8,128)(2,1)S(1)}, bf16[64,1024]{1,0:T(8,128)(2,1)S(1)}, u32[]{:S(2)}, u32[]{:S(2)}) collective-permute-start(bf16[64,1024]{1,0:T(8,128)(2,1)S(1)} %activate.3.refs_0_), channel_id=1, source_target_pairs={{0,4},{4,8},{8,12},{12,0},{1,5},{5,9},{9,13},{13,1},{2,6},{6,10},{... | collective-permute-start | bytes 393224 | tf_op jit(solution)/shard_map/ppermute | solution.py:181
  131.5 2.3 %collective-permute-start.34 = (bf16[64,1024]{1,0:T(8,128)(2,1)S(1)}, bf16[64,1024]{1,0:T(8,128)(2,1)S(1)}, u32[]{:S(2)}, u32[]{:S(2)}) collective-permute-start(bf16[64,1024]{1,0:T(8,128)(2,1)S(1)} %activate.3.refs_0_), channel_id=1, source_target_pairs={{0,8},{4,12},{8,0},{12,4},{1,9},{5,13},{9,1},{13,5},{2,10},{6,14},... | collective-permute-start | bytes 393224 | tf_op jit(solution)/shard_map/ppermute | solution.py:181
  133.8 1.6 collective-permute-start.35
  135.5 1.3 collective-permute-done.33.refs_1_
  136.8 13.2 %collective-permute-done.34.refs_2_ = bf16[64,1024]{1,0:T(8,128)(2,1)S(1)} collective-permute-done((bf16[64,1024]{1,0:T(8,128)(2,1)S(1)}, bf16[64,1024]{1,0:T(8,128)(2,1)S(1)}, u32[]{:S(2)}, u32[]{:S(2)}) %collective-permute-start.34) | collective-permute-done | bytes 131104 | tf_op jit(solution)/shard_map/ppermute | solution.py:181
  151.3 2.8 %collective-permute-start.24 = (bf16[64,768]{1,0:T(8,128)(2,1)S(1)}, bf16[64,768]{1,0:T(8,128)(2,1)S(1)}, u32[]{:S(2)}, u32[]{:S(2)}) collective-permute-start(bf16[64,768]{1,0:T(8,128)(2,1)S(1)} %activate.2.refs_0_), channel_id=1, source_target_pairs={{0,4},{4,8},{8,12},{12,0},{1,5},{5,9},{9,13},{13,1},{2,6},{6,10},{... | collective-permute-start | bytes 294920 | tf_op jit(solution)/shard_map/ppermute | solution.py:181
  154.1 1.5 collective-permute-start.25
  155.6 0.9 collective-permute-start.26
  158.5 3.8 %collective-permute-done.25.refs_2_ = bf16[64,768]{1,0:T(8,128)(2,1)S(1)} collective-permute-done((bf16[64,768]{1,0:T(8,128)(2,1)S(1)}, bf16[64,768]{1,0:T(8,128)(2,1)S(1)}, u32[]{:S(2)}, u32[]{:S(2)}) %collective-permute-start.25) | collective-permute-done | bytes 98336 | tf_op jit(solution)/shard_map/ppermute | solution.py:181
  162.8 1.8 %down.2.refs_8_ = f32[128,1024]{1,0:T(8,128)S(1)} custom-call(s32[6]{0:T(128)S(1)} %stack.114.scal_ref, bf16[64,1024]{1,0:T(8,128)(2,1)S(1)} %activate.3.refs_0_, bf16[64,1024]{1,0:T(8,128)(2,1)S(1)} %collective-permute-done.33.refs_1_, bf16[64,1024]{1,0:T(8,128)(2,1)S(1)} %collective-permute-done.34.refs_2_, ...), custom_call_target="tpu_custom_call" | custom-call | flops 1073741824 | bytes 8388608 | tf_op jit(solution)/shard_map/down/pallas_call | solution.py:694
  164.7 1.7 down.3
  166.4 1.5 collective-permute-start.40
  167.9 4.0 %collective-permute-done.40 = bf16[64,1024]{1,0:T(8,128)(2,1)S(1)} collective-permute-done((bf16[64,1024]{1,0:T(8,128)(2,1)S(1)}, bf16[64,1024]{1,0:T(8,128)(2,1)S(1)}, u32[]{:S(2)}, u32[]{:S(2)}) %collective-permute-start.40) | collective-permute-done | bytes 131104 | tf_op jit(solution)/shard_map/ppermute | solution.py:186
  (103 shorter events, 10.5 us)
Async XLA Ops:
  0.0 14.4 %collective-permute-start.1 = (bf16[3072,512]{1,0:T(8,128)(2,1)}, bf16[3072,512]{1,0:T(8,128)(2,1)}, u32[]{:S(2)}, u32[]{:S(2)}) collective-permute-start(bf16[3072,512]{1,0:T(8,128)(2,1)} %refs_0_.7), channel_id=1, source_target_pairs={{0,1},{1,0},{2,3},{3,2},{4,5},{5,4},{6,7},{7,6},{8,9},{9,8},{10,11... | collective-permute-start | bytes 9437192 | tf_op jit(solution)/shard_map/ppermute | solution.py:186
  0.6 13.8 %collective-permute-start.2 = (bf16[3072,512]{1,0:T(8,128)(2,1)}, bf16[3072,512]{1,0:T(8,128)(2,1)}, u32[]{:S(2)}, u32[]{:S(2)}) collective-permute-start(bf16[3072,512]{1,0:T(8,128)(2,1)} %refs_1_.7), channel_id=1, source_target_pairs={{0,1},{1,0},{2,3},{3,2},{4,5},{5,4},{6,7},{7,6},{8,9},{9,8},{10,11... | collective-permute-start | bytes 9437192 | tf_op jit(solution)/shard_map/ppermute | solution.py:186
  2.4 11.9 %collective-permute-start = (bf16[32,2048]{1,0:T(8,128)(2,1)S(1)}, bf16[32,2048]{1,0:T(8,128)(2,1)S(1)}, u32[]{:S(2)}, u32[]{:S(2)}) collective-permute-start(bf16[32,2048]{1,0:T(8,128)(2,1)S(1)} %constant_dynamic-slice_fusion.q_ref), channel_id=1, source_target_pairs={{0,4},{4,8},{8,12},{12,0},{1,5},{5,9},{9,13},{13,1},{2,6},{6,10},{... | collective-permute-start | bytes 393224 | tf_op jit(solution)/shard_map/ppermute | solution.py:181
  5.4 19.6 %collective-permute-start.4 = (bf16[32,2048]{1,0:T(8,128)(2,1)S(1)}, bf16[32,2048]{1,0:T(8,128)(2,1)S(1)}, u32[]{:S(2)}, u32[]{:S(2)}) collective-permute-start(bf16[32,2048]{1,0:T(8,128)(2,1)S(1)} %constant_dynamic-slice_fusion.q_ref), channel_id=1, source_target_pairs={{0,12},{4,0},{8,4},{12,8},{1,13},{5,1},{9,5},{13,9},{2,14},{6,2},{... | collective-permute-start | bytes 393224 | tf_op jit(solution)/shard_map/ppermute | solution.py:181
  7.5 26.4 %collective-permute-start.6 = (bf16[32,2048]{1,0:T(8,128)(2,1)S(1)}, bf16[32,2048]{1,0:T(8,128)(2,1)S(1)}, u32[]{:S(2)}, u32[]{:S(2)}) collective-permute-start(bf16[32,2048]{1,0:T(8,128)(2,1)S(1)} %constant_dynamic-slice_fusion.q_ref), channel_id=1, source_target_pairs={{0,8},{4,12},{8,0},{12,4},{1,9},{5,13},{9,1},{13,5},{2,10},{6,14},... | collective-permute-start | bytes 393224 | tf_op jit(solution)/shard_map/ppermute | solution.py:181
  25.0 20.9 %collective-permute-start.3 = (bf16[528,128]{1,0:T(8,128)(2,1)S(1)}, bf16[528,128]{1,0:T(8,128)(2,1)S(1)}, u32[]{:S(2)}, u32[]{:S(2)}) collective-permute-start(bf16[528,128]{1,0:T(8,128)(2,1)S(1)} %attend.6), channel_id=1, source_target_pairs={{0,12},{4,0},{8,4},{12,8},{1,13},{5,1},{9,5},{13,9},{2,14},{6,2},{... | collective-permute-start | bytes 405512 | tf_op jit(solution)/shard_map/ppermute | solution.py:181
  25.1 37.1 %slice-start.4 = ((s8[8388608]{0:T(1024)(128)(4,1)}), s8[4194304]{0:T(1024)(128)(4,1)S(1)}, s32[]{:S(2)}) async-start(s8[8388608]{0:T(1024)(128)(4,1)} %bitcast.22), calls=%async_computation.4 | async-start | bytes 8388608
  31.9 30.2 %slice-start.5 = ((s8[8388608]{0:T(1024)(128)(4,1)}), s8[4194304]{0:T(1024)(128)(4,1)S(1)}, s32[]{:S(2)}) async-start(s8[8388608]{0:T(1024)(128)(4,1)} %bitcast.22), calls=%async_computation.5 | async-start | bytes 8388608
  31.9 14.0 %collective-permute-start.5 = (bf16[528,128]{1,0:T(8,128)(2,1)S(1)}, bf16[528,128]{1,0:T(8,128)(2,1)S(1)}, u32[]{:S(2)}, u32[]{:S(2)}) collective-permute-start(bf16[528,128]{1,0:T(8,128)(2,1)S(1)} %attend.7), channel_id=1, source_target_pairs={{0,4},{4,8},{8,12},{12,0},{1,5},{5,9},{9,13},{13,1},{2,6},{6,10},{... | collective-permute-start | bytes 405512 | tf_op jit(solution)/shard_map/ppermute | solution.py:181
  41.0 7.8 %collective-permute-start.7 = (bf16[528,128]{1,0:T(8,128)(2,1)S(1)}, bf16[528,128]{1,0:T(8,128)(2,1)S(1)}, u32[]{:S(2)}, u32[]{:S(2)}) collective-permute-start(bf16[528,128]{1,0:T(8,128)(2,1)S(1)} %attend.8), channel_id=1, source_target_pairs={{0,8},{4,12},{8,0},{12,4},{1,9},{5,13},{9,1},{13,5},{2,10},{6,14},... | collective-permute-start | bytes 405512 | tf_op jit(solution)/shard_map/ppermute | solution.py:181
  49.2 8.2 %collective-permute-start.8 = (bf16[32,2048]{1,0:T(8,128)(2,1)S(1)}, bf16[32,2048]{1,0:T(8,128)(2,1)S(1)}, u32[]{:S(2)}, u32[]{:S(2)}) collective-permute-start(bf16[32,2048]{1,0:T(8,128)(2,1)S(1)} %merge.1.refs_0_), channel_id=1, source_target_pairs={{0,4},{4,8},{8,12},{12,0},{1,5},{5,9},{9,13},{13,1},{2,6},{6,10},{... | collective-permute-start | bytes 393224 | tf_op jit(solution)/shard_map/ppermute | solution.py:181
  49.2 12.4 %collective-permute-start.9 = (bf16[32,2048]{1,0:T(8,128)(2,1)S(1)}, bf16[32,2048]{1,0:T(8,128)(2,1)S(1)}, u32[]{:S(2)}, u32[]{:S(2)}) collective-permute-start(bf16[32,2048]{1,0:T(8,128)(2,1)S(1)} %merge.1.refs_0_), channel_id=1, source_target_pairs={{0,8},{4,12},{8,0},{12,4},{1,9},{5,13},{9,1},{13,5},{2,10},{6,14},... | collective-permute-start | bytes 393224 | tf_op jit(solution)/shard_map/ppermute | solution.py:181
  50.1 11.5 %collective-permute-start.10 = (bf16[32,2048]{1,0:T(8,128)(2,1)S(1)}, bf16[32,2048]{1,0:T(8,128)(2,1)S(1)}, u32[]{:S(2)}, u32[]{:S(2)}) collective-permute-start(bf16[32,2048]{1,0:T(8,128)(2,1)S(1)} %merge.1.refs_0_), channel_id=1, source_target_pairs={{0,12},{4,0},{8,4},{12,8},{1,13},{5,1},{9,5},{13,9},{2,14},{6,2},{... | collective-permute-start | bytes 393224 | tf_op jit(solution)/shard_map/ppermute | solution.py:181
  53.1 9.7 %collective-permute-start.11 = (bf16[32,2048]{1,0:T(8,128)(2,1)S(1)}, bf16[32,2048]{1,0:T(8,128)(2,1)S(1)}, u32[]{:S(2)}, u32[]{:S(2)}) collective-permute-start(bf16[32,2048]{1,0:T(8,128)(2,1)S(1)} %merge.1.refs_0_), channel_id=1, source_target_pairs={{0,1},{1,0},{2,3},{3,2},{4,5},{5,4},{6,7},{7,6},{8,9},{9,8},{10,11... | collective-permute-start | bytes 393224 | tf_op jit(solution)/shard_map/ppermute | solution.py:186
  57.4 5.4 %collective-permute-start.12 = (bf16[32,2048]{1,0:T(8,128)(2,1)S(1)}, bf16[32,2048]{1,0:T(8,128)(2,1)S(1)}, u32[]{:S(2)}, u32[]{:S(2)}) collective-permute-start(bf16[32,2048]{1,0:T(8,128)(2,1)S(1)} %collective-permute-done.8.refs_1_), channel_id=1, source_target_pairs={{0,1},{1,0},{2,3},{3,2},{4,5},{5,4},{6,7},{7,6},{8,9},{9,8},{10,11... | collective-permute-start | bytes 393224 | tf_op jit(solution)/shard_map/ppermute | solution.py:186
  61.6 1.3 collective-permute-start.13
  61.6 1.5 collective-permute-start.14
  64.5 6.0 %collective-permute-start.15 = (bf16[128,512]{1,0:T(8,128)(2,1)S(1)}, bf16[128,512]{1,0:T(8,128)(2,1)S(1)}, u32[]{:S(2)}, u32[]{:S(2)}) collective-permute-start(bf16[128,512]{1,0:T(8,128)(2,1)S(1)} %project.2.refs_0_), channel_id=1, source_target_pairs={{0,2},{2,0},{1,3},{3,1},{4,6},{6,4},{5,7},{7,5},{8,10},{10,8},{9,1... | collective-permute-start | bytes 393224 | tf_op jit(solution)/shard_map/ppermute | solution.py:186
  67.3 5.7 %collective-permute-start.16 = (bf16[128,512]{1,0:T(8,128)(2,1)S(1)}, bf16[128,512]{1,0:T(8,128)(2,1)S(1)}, u32[]{:S(2)}, u32[]{:S(2)}) collective-permute-start(bf16[128,512]{1,0:T(8,128)(2,1)S(1)} %project.3.refs_1_), channel_id=1, source_target_pairs={{0,2},{2,0},{1,3},{3,1},{4,6},{6,4},{5,7},{7,5},{8,10},{10,8},{9,1... | collective-permute-start | bytes 393224 | tf_op jit(solution)/shard_map/ppermute | solution.py:186
  82.6 2.7 %collective-permute-start.17 = (bf16[128,4096]{1,0:T(8,128)(2,1)S(1)}, bf16[128,4096]{1,0:T(8,128)(2,1)S(1)}, u32[]{:S(2)}, u32[]{:S(2)}) collective-permute-start(bf16[128,4096]{1,0:T(8,128)(2,1)S(1)} %get-tuple-element.58), channel_id=1, source_target_pairs={{0,1},{1,0},{2,3},{3,2},{4,5},{5,4},{6,7},{7,6},{8,9},{9,8},{10,11... | collective-permute-start | bytes 3145736 | tf_op jit(solution)/shard_map/ppermute | solution.py:186
  85.6 71.0 %slice-start = ((s8[14680064]{0:T(1024)(128)(4,1)}), s8[4194304]{0:T(1024)(128)(4,1)S(1)}, s32[]{:S(2)}) async-start(s8[14680064]{0:T(1024)(128)(4,1)} %bitcast.20), calls=%async_computation | async-start | bytes 8388608
  85.6 70.9 %slice-start.1 = ((s8[14680064]{0:T(1024)(128)(4,1)}), s8[4194304]{0:T(1024)(128)(4,1)S(1)}, s32[]{:S(2)}) async-start(s8[14680064]{0:T(1024)(128)(4,1)} %bitcast.20), calls=%async_computation.1 | async-start | bytes 8388608
  85.6 70.9 %slice-start.2 = ((s8[14680064]{0:T(1024)(128)(4,1)}), s8[4194304]{0:T(1024)(128)(4,1)S(1)}, s32[]{:S(2)}) async-start(s8[14680064]{0:T(1024)(128)(4,1)} %bitcast.20), calls=%async_computation.2 | async-start | bytes 8388608
  85.7 70.9 %slice-start.3 = ((s8[14680064]{0:T(1024)(128)(4,1)}), s8[2097152]{0:T(1024)(128)(4,1)S(1)}, s32[]{:S(2)}) async-start(s8[14680064]{0:T(1024)(128)(4,1)} %bitcast.20), calls=%async_computation.3 | async-start | bytes 4194304
  93.7 2.4 %collective-permute-start.18 = (bf16[128,3072]{1,0:T(8,128)(2,1)S(1)}, bf16[128,3072]{1,0:T(8,128)(2,1)S(1)}, u32[]{:S(2)}, u32[]{:S(2)}) collective-permute-start(bf16[128,3072]{1,0:T(8,128)(2,1)S(1)} %get-tuple-element.62), channel_id=1, source_target_pairs={{0,1},{1,0},{2,3},{3,2},{4,5},{5,4},{6,7},{7,6},{8,9},{9,8},{10,11... | collective-permute-start | bytes 2359304 | tf_op jit(solution)/shard_map/ppermute | solution.py:186
  93.8 14.8 %collective-permute-start.31 = (bf16[128,2048]{1,0:T(8,128)(2,1)S(1)}, bf16[128,2048]{1,0:T(8,128)(2,1)S(1)}, u32[]{:S(2)}, u32[]{:S(2)}) collective-permute-start(bf16[128,2048]{1,0:T(8,128)(2,1)S(1)} %get-tuple-element.70), channel_id=1, source_target_pairs={{0,4},{4,0},{8,12},{12,8},{1,5},{5,1},{9,13},{13,9},{2,6},{6,2},{1... | collective-permute-start | bytes 1572872 | tf_op jit(solution)/shard_map/ppermute | solution.py:186
  96.2 34.6 %collective-permute-start.19 = (bf16[128,1536]{1,0:T(8,128)(2,1)S(1)}, bf16[128,1536]{1,0:T(8,128)(2,1)S(1)}, u32[]{:S(2)}, u32[]{:S(2)}) collective-permute-start(bf16[128,1536]{1,0:T(8,128)(2,1)S(1)} %get-tuple-element.65), channel_id=1, source_target_pairs={{0,4},{4,0},{8,12},{12,8},{1,5},{5,1},{9,13},{13,9},{2,6},{6,2},{1... | collective-permute-start | bytes 1179656 | tf_op jit(solution)/shard_map/ppermute | solution.py:186
  108.8 19.0 %collective-permute-start.32 = (bf16[128,1024]{1,0:T(8,128)(2,1)S(1)}, bf16[128,1024]{1,0:T(8,128)(2,1)S(1)}, u32[]{:S(2)}, u32[]{:S(2)}) collective-permute-start(bf16[128,1024]{1,0:T(8,128)(2,1)S(1)} %get-tuple-element.72), channel_id=1, source_target_pairs={{0,8},{4,12},{8,0},{12,4},{1,9},{5,13},{9,1},{13,5},{2,10},{6,14},... | collective-permute-start | bytes 786440 | tf_op jit(solution)/shard_map/ppermute | solution.py:186
  109.9 12.2 %collective-permute-start.21 = (f32[8,128]{1,0:T(8,128)S(1)}, f32[8,128]{1,0:T(8,128)S(1)}, u32[]{:S(2)}, u32[]{:S(2)}) collective-permute-start(f32[8,128]{1,0:T(8,128)S(1)} %get-tuple-element.68), channel_id=1, source_target_pairs={{0,4},{4,0},{8,12},{12,8},{1,5},{5,1},{9,13},{13,9},{2,6},{6,2},{1... | collective-permute-start | bytes 12296 | tf_op jit(solution)/shard_map/ppermute | solution.py:186
  122.1 4.5 %collective-permute-start.22 = (f32[8,128]{1,0:T(8,128)S(1)}, f32[8,128]{1,0:T(8,128)S(1)}, u32[]{:S(2)}, u32[]{:S(2)}) collective-permute-start(f32[8,128]{1,0:T(8,128)S(1)} %add.117), channel_id=1, source_target_pairs={{0,8},{4,12},{8,0},{12,4},{1,9},{5,13},{9,1},{13,5},{2,10},{6,14},... | collective-permute-start | bytes 12296 | tf_op jit(solution)/shard_map/ppermute | solution.py:186
  126.6 1.2 collective-permute-start.23
  128.5 8.3 %collective-permute-start.33 = (bf16[64,1024]{1,0:T(8,128)(2,1)S(1)}, bf16[64,1024]{1,0:T(8,128)(2,1)S(1)}, u32[]{:S(2)}, u32[]{:S(2)}) collective-permute-start(bf16[64,1024]{1,0:T(8,128)(2,1)S(1)} %activate.3.refs_0_), channel_id=1, source_target_pairs={{0,4},{4,8},{8,12},{12,0},{1,5},{5,9},{9,13},{13,1},{2,6},{6,10},{... | collective-permute-start | bytes 393224 | tf_op jit(solution)/shard_map/ppermute | solution.py:181
  130.8 19.7 %collective-permute-start.20 = (bf16[128,768]{1,0:T(8,128)(2,1)S(1)}, bf16[128,768]{1,0:T(8,128)(2,1)S(1)}, u32[]{:S(2)}, u32[]{:S(2)}) collective-permute-start(bf16[128,768]{1,0:T(8,128)(2,1)S(1)} %get-tuple-element.67), channel_id=1, source_target_pairs={{0,8},{4,12},{8,0},{12,4},{1,9},{5,13},{9,1},{13,5},{2,10},{6,14},... | collective-permute-start | bytes 589832 | tf_op jit(solution)/shard_map/ppermute | solution.py:186
  131.5 18.5 %collective-permute-start.34 = (bf16[64,1024]{1,0:T(8,128)(2,1)S(1)}, bf16[64,1024]{1,0:T(8,128)(2,1)S(1)}, u32[]{:S(2)}, u32[]{:S(2)}) collective-permute-start(bf16[64,1024]{1,0:T(8,128)(2,1)S(1)} %activate.3.refs_0_), channel_id=1, source_target_pairs={{0,8},{4,12},{8,0},{12,4},{1,9},{5,13},{9,1},{13,5},{2,10},{6,14},... | collective-permute-start | bytes 393224 | tf_op jit(solution)/shard_map/ppermute | solution.py:181
  133.8 16.2 %collective-permute-start.35 = (bf16[64,1024]{1,0:T(8,128)(2,1)S(1)}, bf16[64,1024]{1,0:T(8,128)(2,1)S(1)}, u32[]{:S(2)}, u32[]{:S(2)}) collective-permute-start(bf16[64,1024]{1,0:T(8,128)(2,1)S(1)} %activate.3.refs_0_), channel_id=1, source_target_pairs={{0,12},{4,0},{8,4},{12,8},{1,13},{5,1},{9,5},{13,9},{2,14},{6,2},{... | collective-permute-start | bytes 393224 | tf_op jit(solution)/shard_map/ppermute | solution.py:181
  135.5 18.7 %collective-permute-start.36 = (bf16[64,1024]{1,0:T(8,128)(2,1)S(1)}, bf16[64,1024]{1,0:T(8,128)(2,1)S(1)}, u32[]{:S(2)}, u32[]{:S(2)}) collective-permute-start(bf16[64,1024]{1,0:T(8,128)(2,1)S(1)} %activate.3.refs_0_), channel_id=1, source_target_pairs={{0,1},{1,0},{2,3},{3,2},{4,5},{5,4},{6,7},{7,6},{8,9},{9,8},{10,11... | collective-permute-start | bytes 393224 | tf_op jit(solution)/shard_map/ppermute | solution.py:186
  136.8 18.8 %collective-permute-start.37 = (bf16[64,1024]{1,0:T(8,128)(2,1)S(1)}, bf16[64,1024]{1,0:T(8,128)(2,1)S(1)}, u32[]{:S(2)}, u32[]{:S(2)}) collective-permute-start(bf16[64,1024]{1,0:T(8,128)(2,1)S(1)} %collective-permute-done.33.refs_1_), channel_id=1, source_target_pairs={{0,1},{1,0},{2,3},{3,2},{4,5},{5,4},{6,7},{7,6},{8,9},{9,8},{10,11... | collective-permute-start | bytes 393224 | tf_op jit(solution)/shard_map/ppermute | solution.py:186
  150.1 7.6 %collective-permute-start.38 = (bf16[64,1024]{1,0:T(8,128)(2,1)S(1)}, bf16[64,1024]{1,0:T(8,128)(2,1)S(1)}, u32[]{:S(2)}, u32[]{:S(2)}) collective-permute-start(bf16[64,1024]{1,0:T(8,128)(2,1)S(1)} %collective-permute-done.34.refs_2_), channel_id=1, source_target_pairs={{0,1},{1,0},{2,3},{3,2},{4,5},{5,4},{6,7},{7,6},{8,9},{9,8},{10,11... | collective-permute-start | bytes 393224 | tf_op jit(solution)/shard_map/ppermute | solution.py:186
  150.1 12.8 %collective-permute-start.39 = (bf16[64,1024]{1,0:T(8,128)(2,1)S(1)}, bf16[64,1024]{1,0:T(8,128)(2,1)S(1)}, u32[]{:S(2)}, u32[]{:S(2)}) collective-permute-start(bf16[64,1024]{1,0:T(8,128)(2,1)S(1)} %collective-permute-done.35.refs_3_), channel_id=1, source_target_pairs={{0,1},{1,0},{2,3},{3,2},{4,5},{5,4},{6,7},{7,6},{8,9},{9,8},{10,11... | collective-permute-start | bytes 393224 | tf_op jit(solution)/shard_map/ppermute | solution.py:186
  151.3 7.2 %collective-permute-start.24 = (bf16[64,768]{1,0:T(8,128)(2,1)S(1)}, bf16[64,768]{1,0:T(8,128)(2,1)S(1)}, u32[]{:S(2)}, u32[]{:S(2)}) collective-permute-start(bf16[64,768]{1,0:T(8,128)(2,1)S(1)} %activate.2.refs_0_), channel_id=1, source_target_pairs={{0,4},{4,8},{8,12},{12,0},{1,5},{5,9},{9,13},{13,1},{2,6},{6,10},{... | collective-permute-start | bytes 294920 | tf_op jit(solution)/shard_map/ppermute | solution.py:181
  154.1 8.2 %collective-permute-start.25 = (bf16[64,768]{1,0:T(8,128)(2,1)S(1)}, bf16[64,768]{1,0:T(8,128)(2,1)S(1)}, u32[]{:S(2)}, u32[]{:S(2)}) collective-permute-start(bf16[64,768]{1,0:T(8,128)(2,1)S(1)} %activate.2.refs_0_), channel_id=1, source_target_pairs={{0,8},{4,12},{8,0},{12,4},{1,9},{5,13},{9,1},{13,5},{2,10},{6,14},... | collective-permute-start | bytes 294920 | tf_op jit(solution)/shard_map/ppermute | solution.py:181
  155.6 6.7 %collective-permute-start.26 = (bf16[64,768]{1,0:T(8,128)(2,1)S(1)}, bf16[64,768]{1,0:T(8,128)(2,1)S(1)}, u32[]{:S(2)}, u32[]{:S(2)}) collective-permute-start(bf16[64,768]{1,0:T(8,128)(2,1)S(1)} %activate.2.refs_0_), channel_id=1, source_target_pairs={{0,12},{4,0},{8,4},{12,8},{1,13},{5,1},{9,5},{13,9},{2,14},{6,2},{... | collective-permute-start | bytes 294920 | tf_op jit(solution)/shard_map/ppermute | solution.py:181
  157.2 15.4 %copy-start.1 = (bf16[32,4096]{1,0:T(8,128)(2,1)S(1)}, bf16[32,4096]{1,0:T(8,128)(2,1)}, u32[]{:S(2)}) copy-start(bf16[32,4096]{1,0:T(8,128)(2,1)} %param.11) | copy-start | bytes 786436
  157.7 7.0 %collective-permute-start.27 = (bf16[64,768]{1,0:T(8,128)(2,1)S(1)}, bf16[64,768]{1,0:T(8,128)(2,1)S(1)}, u32[]{:S(2)}, u32[]{:S(2)}) collective-permute-start(bf16[64,768]{1,0:T(8,128)(2,1)S(1)} %activate.2.refs_0_), channel_id=1, source_target_pairs={{0,1},{1,0},{2,3},{3,2},{4,5},{5,4},{6,7},{7,6},{8,9},{9,8},{10,11... | collective-permute-start | bytes 294920 | tf_op jit(solution)/shard_map/ppermute | solution.py:186
  158.5 6.2 %collective-permute-start.28 = (bf16[64,768]{1,0:T(8,128)(2,1)S(1)}, bf16[64,768]{1,0:T(8,128)(2,1)S(1)}, u32[]{:S(2)}, u32[]{:S(2)}) collective-permute-start(bf16[64,768]{1,0:T(8,128)(2,1)S(1)} %collective-permute-done.24.refs_1_), channel_id=1, source_target_pairs={{0,1},{1,0},{2,3},{3,2},{4,5},{5,4},{6,7},{7,6},{8,9},{9,8},{10,11... | collective-permute-start | bytes 294920 | tf_op jit(solution)/shard_map/ppermute | solution.py:186
  162.3 2.4 %collective-permute-start.29 = (bf16[64,768]{1,0:T(8,128)(2,1)S(1)}, bf16[64,768]{1,0:T(8,128)(2,1)S(1)}, u32[]{:S(2)}, u32[]{:S(2)}) collective-permute-start(bf16[64,768]{1,0:T(8,128)(2,1)S(1)} %collective-permute-done.25.refs_2_), channel_id=1, source_target_pairs={{0,1},{1,0},{2,3},{3,2},{4,5},{5,4},{6,7},{7,6},{8,9},{9,8},{10,11... | collective-permute-start | bytes 294920 | tf_op jit(solution)/shard_map/ppermute | solution.py:186
  162.3 2.4 %collective-permute-start.30 = (bf16[64,768]{1,0:T(8,128)(2,1)S(1)}, bf16[64,768]{1,0:T(8,128)(2,1)S(1)}, u32[]{:S(2)}, u32[]{:S(2)}) collective-permute-start(bf16[64,768]{1,0:T(8,128)(2,1)S(1)} %collective-permute-done.26.refs_3_), channel_id=1, source_target_pairs={{0,1},{1,0},{2,3},{3,2},{4,5},{5,4},{6,7},{7,6},{8,9},{9,8},{10,11... | collective-permute-start | bytes 294920 | tf_op jit(solution)/shard_map/ppermute | solution.py:186
  166.4 5.5 %collective-permute-start.40 = (bf16[64,1024]{1,0:T(8,128)(2,1)S(1)}, bf16[64,1024]{1,0:T(8,128)(2,1)S(1)}, u32[]{:S(2)}, u32[]{:S(2)}) collective-permute-start(bf16[64,1024]{1,0:T(8,128)(2,1)S(1)} %get-tuple-element.74), channel_id=1, source_target_pairs={{0,2},{2,0},{1,3},{3,1},{4,6},{6,4},{5,7},{7,5},{8,10},{10,8},{9,1... | collective-permute-start | bytes 393224 | tf_op jit(solution)/shard_map/ppermute | solution.py:186
  (10 other events, 78.6 us)
where the time goes:
time: 173 us
  waiting for transfers between devices  68 us (39%)
  Pallas kernels  59.2 us (34%)
  starting transfers between devices  38.7 us (22%)
  local copies, waits for them, and re-layouts  4.04 us (2%)
    ppermute x26, waiting for transfers between devices, exchanged(): return lax.ppermute(value, axis, [(i, i ^ bit) for i in range(devices)])  37.5 us
    pallas_call x5, Pallas kernels, attend_block(): pl.pallas_call(functools.partial(attention_kernel, sources=len(sources),...  31.3 us
    ppermute x15, waiting for transfers between devices, rotation(): lax.ppermute(value, axis, [(i, (i + by) % devices) for i in range(devices)])  30.4 us
    ppermute x15, starting transfers between devices, rotation(): lax.ppermute(value, axis, [(i, (i + by) % devices) for i in range(devices)])  23.6 us
    pallas_call x2, Pallas kernels, gate_up_part(): pl.pallas_call(gate_up_kernel, grid=(count // tile,), out_shape=(out, out...  16.5 us
    ppermute x26, starting transfers between devices, exchanged(): return lax.ppermute(value, axis, [(i, i ^ bit) for i in range(devices)])  15.1 us
    unnamed x34, local copies, waits for them, and re-layouts  3.86 us
    pallas_call x2, Pallas kernels, down_project(): pl.pallas_call(functools.partial(down_kernel, pieces=pieces, last=last),...  3.5 us
  transfers between devices with their start and end apart: 41, of which 18 were waited for; matrix products, arithmetic and copies ran while one was open for 1% of the time, Pallas kernels for 22%

commit v1 on v0

--- a/solution.py
+++ b/solution.py
@@ -17,7 +17,7 @@
 
 NEG = -1e30
 EPSILON = 1e-05
-STREAMS = (4, 3)
+STREAMS = (2, 3, 2)
 SLABS = 2
 
 
@@ -168,15 +168,15 @@
 LOG2E = 1.4426950408889634
 PIECES = 3
 STAT_ROWS = 16
+MOST_KEYS = 4096
 SMALL = 8 * 2**20
 MEDIUM = 16 * 2**20
 LARGE = 28 * 2**20
-ALONE = 61 * 2**20
 LOADING = 12 * 2**20
 LANES = 4
 
 
-def rotation(value, axis, by):
+def rotated(value, axis, by):
     devices = lax.axis_size(axis)
     return lax.ppermute(value, axis, [(i, (i + by) % devices) for i in range(devices)])
 
@@ -216,7 +216,7 @@
     )
 
 
-def attention_kernel(scal_ref, q_ref, nk_ref, nv_ref, *refs, sources, chunk, group_size, with_new):
+def attention_kernel(scal_ref, q_ref, nk_ref, nv_ref, *refs, sources, chunk, group_size):
     out_ref, q_buf, s_buf, max_buf, sum_buf, acc_buf, k_buf, v_buf, k_sems, v_sems = refs[
         2 * sources :
     ]
@@ -228,9 +228,6 @@
     factor = DH ** (-0.5) * LOG2E
     first = scal_ref[sources + 1]
 
-    def columns(j):
-        return pl.ds(pl.multiple_of((first + j) * DH, DH), DH)
-
     def copy_of(i, c, which):
         buffer, sems = ((k_buf, k_sems), (v_buf, v_sems))[which]
         return pltpu.make_async_copy(
@@ -258,20 +255,19 @@
     sum_buf[...] = jnp.zeros(sum_buf.shape, jnp.float32)
     acc_buf[...] = jnp.zeros(acc_buf.shape, jnp.float32)
     new_scores = []
-    if with_new:
-        shape = (rows, nk_ref.shape[0])
-        new_masks = (
-            lax.broadcasted_iota(jnp.int32, shape, 1)
-            <= lax.broadcasted_iota(jnp.int32, shape, 0) % rows_in + scal_ref[sources]
-        )
-        for j in range(groups):
-            fresh = lax.dot_general(
-                q_buf[j],
-                nk_ref[:, columns(j)],
-                (((1,), (1,)), ((), ())),
-                preferred_element_type=jnp.float32,
-            )
-            new_scores.append(jnp.where(new_masks, fresh, NEG))
+    shape = (rows, nk_ref.shape[0])
+    new_masks = (
+        lax.broadcasted_iota(jnp.int32, shape, 1)
+        <= lax.broadcasted_iota(jnp.int32, shape, 0) % rows_in + scal_ref[sources]
+    )
+    for j in range(groups):
+        fresh = lax.dot_general(
+            q_buf[j],
+            nk_ref[:, j * DH : (j + 1) * DH],
+            (((1,), (1,)), ((), ())),
+            preferred_element_type=jnp.float32,
+        )
+        new_scores.append(jnp.where(new_masks, fresh, NEG))
 
     def wait_for(u, which):
         buffer, sems = ((k_buf, k_sems), (v_buf, v_sems))[which]
@@ -320,8 +316,7 @@
     peaks = []
     for j in range(groups):
         peak = jnp.max(max_buf[j], axis=1, keepdims=True)
-        if with_new:
-            peak = jnp.maximum(peak, jnp.max(new_scores[j], axis=1, keepdims=True))
+        peak = jnp.maximum(peak, jnp.max(new_scores[j], axis=1, keepdims=True))
         peaks.append(peak * factor)
 
     def weights_step(u, carry):
@@ -350,14 +345,13 @@
     for j in range(groups):
         total = jnp.sum(sum_buf[j], axis=1, keepdims=True)
         summed = acc_buf[j]
-        if with_new:
-            weights = jnp.where(new_masks, jnp.exp2(new_scores[j] * factor - peaks[j]), 0.0)
-            total = total + jnp.sum(weights, axis=1, keepdims=True)
-            summed = summed + jnp.dot(
-                weights.astype(jnp.bfloat16),
-                nv_ref[:, columns(j)],
-                preferred_element_type=jnp.float32,
-            )
+        weights = jnp.where(new_masks, jnp.exp2(new_scores[j] * factor - peaks[j]), 0.0)
+        total = total + jnp.sum(weights, axis=1, keepdims=True)
+        summed = summed + jnp.dot(
+            weights.astype(jnp.bfloat16),
+            nv_ref[:, j * DH : (j + 1) * DH],
+            preferred_element_type=jnp.float32,
+        )
         filled = total > 0.0
         safe = jnp.where(filled, total, 1.0)
         lse = jnp.where(filled, peaks[j] + jnp.log(safe) * LOG2E, NEG)
@@ -482,13 +476,15 @@
     out_ref[...] = (gate / (1.0 + jnp.exp(-gate)) * up).astype(jnp.bfloat16)
 
 
-def down_kernel(scal_ref, *refs, pieces, last):
+def down_kernel(scal_ref, *refs, pieces, first, last):
     mine, other = refs[:pieces], refs[pieces : 2 * pieces]
     rest = refs[2 * pieces :]
     core = scal_ref[0]
     half, part = mine[0].shape
+    if not first:
+        before_ref, *rest = rest
     if last:
-        before_ref, weight_ref, keep_ref, send_ref, left_buf, out_buf = rest
+        weight_ref, keep_ref, send_ref, left_buf, out_buf = rest
     else:
         weight_ref, out_ref, left_buf = rest
     for s in range(pieces):
@@ -496,11 +492,13 @@
         left_buf[pl.ds(pl.multiple_of(core * half, half), half), span] = mine[s][...]
         left_buf[pl.ds(pl.multiple_of((1 - core) * half, half), half), span] = other[s][...]
     product = jnp.dot(left_buf[...], weight_ref[...], preferred_element_type=jnp.float32)
+    if not first:
+        product = before_ref[...] + product
     if not last:
         out_ref[...] = product
         return
     side = scal_ref[1]
-    out_buf[...] = before_ref[...] + product
+    out_buf[...] = product
     keep_ref[...] = out_buf[pl.ds(pl.multiple_of(side * half, half), half), :]
     send_ref[...] = out_buf[pl.ds(pl.multiple_of((1 - side) * half, half), half), :].astype(
         jnp.bfloat16
@@ -552,12 +550,16 @@
     return pl.CostEstimate(flops=int(flops), bytes_accessed=int(size), transcendentals=0)
 
 
-def attend_block(scal, with_new, queries, sources, new_keys, new_values, group_size):
+def attend_block(scal, queries, sources, new_keys, new_values, group_size):
     length, width = sources[0][0].shape
     rows_in = queries.shape[0]
     groups = width // DH // 2
     rows = rows_in * group_size
-    chunk = next(c for c in (1536, 1024, 512, 256, 128) if length % c == 0)
+    chunk = next(
+        length // n
+        for n in range(1, length + 1)
+        if length % n == 0 and length // n % 128 == 0 and length // n <= MOST_KEYS
+    )
     keys = len(sources) * length
     return pl.pallas_call(
         functools.partial(
@@ -565,7 +567,6 @@
             sources=len(sources),
             chunk=chunk,
             group_size=group_size,
-            with_new=with_new,
         ),
         out_shape=jax.ShapeDtypeStruct((groups * rows + STAT_ROWS, DH), jnp.bfloat16),
         in_specs=[smem()] + [vmem()] * 3 + [far()] * (2 * len(sources)),
@@ -581,7 +582,7 @@
             pltpu.SemaphoreType.DMA((keys // chunk,)),
             pltpu.SemaphoreType.DMA((keys // chunk,)),
         ],
-        compiler_params=pltpu.CompilerParams(vmem_limit_bytes=ALONE if with_new and len(sources) == 1 else LARGE),
+        compiler_params=pltpu.CompilerParams(vmem_limit_bytes=LARGE),
         cost_estimate=cost(4 * groups * rows * keys * DH * 3, 4 * keys * width),
         name="attend",
     )(scal, queries, new_keys, new_values, *[a for pair in sources for a in pair])
@@ -674,12 +675,12 @@
     )(scal, own, other, squares)
 
 
-def down_project(scal, mine, other, weight, before):
+def down_project(scal, mine, other, weight, before, last):
     pieces = len(mine)
     half, _ = mine[0].shape
     depth, width = weight.shape
-    last = before is not None
-    inputs = [*mine, *other] + ([before] if last else [])
+    first = before is None
+    inputs = [*mine, *other] + ([] if first else [before])
     scratch = [pltpu.VMEM((2 * half, depth), jnp.bfloat16)]
     if last:
         out_shape = (
@@ -692,7 +693,7 @@
         out_shape = jax.ShapeDtypeStruct((2 * half, width), jnp.float32)
         out_specs = vmem()
     return pl.pallas_call(
-        functools.partial(down_kernel, pieces=pieces, last=last),
+        functools.partial(down_kernel, pieces=pieces, first=first, last=last),
         in_specs=[smem()] + [vmem()] * (len(inputs) + 1),
         out_specs=out_specs,
         scratch_shapes=scratch,
@@ -730,6 +731,14 @@
 def half_of(value, which, axis=1):
     size = value.shape[axis] // 2
     return lax.dynamic_slice_in_dim(value, which * size, size, axis)
+
+
+def spread(value, bits):
+    pieces = {0: value}
+    for bit in reversed(bits):
+        for mask in list(pieces):
+            pieces[mask | bit] = exchanged(pieces[mask], "ctx", bit)
+    return [pieces[mask] for mask in range(len(pieces))]
 
 
 def on_device_line(
@@ -757,7 +766,7 @@
         for c in (core, 1 - core)
     )
     bits = [1 << b for b in range(devices.bit_length() - 1)]
-    sources = [(place - s) % devices for s in range(devices)]
+    sources = [place ^ mask for mask in range(devices)]
     blocks = [
         sum((source // bit) % 2 * (devices // (2 * bit)) for bit in bits) for source in sources
     ]
@@ -769,45 +778,36 @@
 
     early = (
         half_of(queries, core),
-        packed(mine_valid, 0, core * groups),
-        packed(other_valid, 0, core * groups),
-        [packed(mine_valid, other_valid, o, core * groups) for o in offsets[1:]],
-        packed(core, *sources),
+        half_of(new_keys, core),
+        half_of(new_values, core),
+        [packed(mine_valid, other_valid, o, core * groups) for o in offsets],
+        packed(core, *((place - s) % devices for s in range(devices))),
         packed(core, side),
         packed(core, side, *blocks),
         [packed((place // bit) % 2) for bit in bits],
     )
     early = lax.optimization_barrier(early)
-    q_mine, own_scal, rest_scal, visit_scals, source_scal, core_scal, down_scal, bit_scals = early
-    order = sorted(range(1, devices), key=lambda s: min(s, devices - s))
-    visiting = {}
-    for s in order:
-        visiting[s] = rotation(q_mine, "ctx", s)
+    q_mine, fresh_keys, fresh_values, visit_scals, source_scal, core_scal, down_scal, bit_scals = early
     k_there = exchanged(cache_keys, "khalf", 1)
     v_there = exchanged(cache_values, "khalf", 1)
-    here, there = (cache_keys, cache_values), (k_there, v_there)
-    last = attend_block(
-        own_scal, True, q_mine, [here], new_keys, new_values, group_size
-    )
-    parts = [last]
-    for s in order:
-        visitor, last = lax.optimization_barrier((visiting[s], last))
+    visiting = spread(q_mine, bits)
+    k_here = loaded(cache_keys, 0, length)
+    v_here = loaded(cache_values, 0, length)
+    here, there = (k_here, v_here), (k_there, v_there)
+    parts = []
+    last = None
+    for mask in [*range(1, devices), 0]:
+        visitor = visiting[mask]
+        if last is not None:
+            visitor, last = lax.optimization_barrier((visitor, last))
         last = attend_block(
-            visit_scals[s - 1],
-            True,
-            visitor,
-            [here, there],
-            new_keys,
-            new_values,
-            group_size,
-        )
-        parts.append(rotation(last, "ctx", -s))
-    q_mine, last = lax.optimization_barrier((q_mine, last))
-    parts.append(attend_block(rest_scal, False, q_mine, [there], new_keys, new_values, group_size))
+            visit_scals[mask], visitor, [here, there], fresh_keys, fresh_values, group_size
+        )
+        parts.append(exchanged(last, "ctx", mask) if mask else last)
     attention = merged(parts, True, rows_in)
-    mine = [attention]
-    for s in range(1, devices):
-        mine.append(rotation(attention, "ctx", s))
+    mine = []
+    for s in range(devices):
+        mine.append(rotated(attention, "ctx", s) if s else attention)
     other = [exchanged(a, "khalf", 1) for a in mine]
     out_near = loaded(out_weight, 0, out_weight.shape[0])
     own, come = [], []
@@ -835,14 +835,11 @@
                 away, left = lax.optimization_barrier((away, left))
             come = exchanged(away, "ctx", bit)
         activated = activate(core_scal, keep, come, squares)
-        mine, other = [], []
-        for s in range(devices):
-            piece = activated
-            if s:
-                piece = rotation(activated, "ctx", s)
-            mine.append(piece)
-            other.append(exchanged(piece, "khalf", 1))
-        down = down_project(down_scal, mine, other, down_near[stream], down)
+        mine = spread(activated, bits)
+        other = [exchanged(piece, "khalf", 1) for piece in mine]
+        down = down_project(
+            down_scal, mine, other, down_near[stream], down, stream == len(STREAMS) - 1
+        )
     keep, send = down
     come = exchanged(send, "kv", 1)
     kept = half_of(hidden, side, 0)

time: 173 us -> 167 us (0.965)
  waiting for transfers between devices: 68 us -> 60.1 us
  starting transfers between devices: 38.7 us -> 44.9 us
  Pallas kernels: 59.2 us -> 55 us
    ppermute x26 -> x48, starting transfers between devices: 15.1 us -> 41.1 us  [exchanged(): return lax.ppermute(value, axis, [(i, i ^ bit) for i in range(devices)])]
    ppermute x15 -> x3, waiting for transfers between devices: 30.4 us -> 7.21 us  [rotated(): lax.ppermute(value, axis, [(i, (i + by) % devices) for i in range(devices)])]
    ppermute x15 -> x3, starting transfers between devices: 23.6 us -> 3.87 us  [rotated(): lax.ppermute(value, axis, [(i, (i + by) % devices) for i in range(devices)])]
    ppermute x26 -> x48, waiting for transfers between devices: 37.5 us -> 52.9 us  [exchanged(): return lax.ppermute(value, axis, [(i, i ^ bit) for i in range(devices)])]
    pallas_call x5 -> x4, Pallas kernels: 31.3 us -> 24.9 us  [attend_block(): pl.pallas_call(functools.partial(attention_kernel, sources=len(sources),...]
    pallas_call x2 -> x3, Pallas kernels: 3.5 us -> 4.21 us  [down_project(): pl.pallas_call(functools.partial(down_kernel, pieces=pieces, first=first,...]
    pallas_call x2 -> x3, Pallas kernels: 16.5 us -> 16.9 us  [gate_up_part(): pl.pallas_call(gate_up_kernel, grid=(count // tile,), out_shape=(out, out...]
    unnamed x34 -> x24, local copies, waits for them, and re-layouts: 3.86 us -> 3.57 us
  transfers between devices with their start and end apart: 41 -> 51, of which waited for: 18 -> 20; matrix products, arithmetic and copies ran while one was open for 1% -> 1% of each run, Pallas kernels for 22% -> 16%
where the time goes in v1:
time: 167 us
  waiting for transfers between devices  60.1 us (36%)
  Pallas kernels  55 us (33%)
  starting transfers between devices  44.9 us (27%)
  local copies, waits for them, and re-layouts  4.5 us (3%)
    ppermute x48, waiting for transfers between devices, exchanged(): return lax.ppermute(value, axis, [(i, i ^ bit) for i in range(devices)])  52.9 us
    ppermute x48, starting transfers between devices, exchanged(): return lax.ppermute(value, axis, [(i, i ^ bit) for i in range(devices)])  41.1 us
    pallas_call x4, Pallas kernels, attend_block(): pl.pallas_call(functools.partial(attention_kernel, sources=len(sources),...  24.9 us
    pallas_call x3, Pallas kernels, gate_up_part(): pl.pallas_call(gate_up_kernel, grid=(count // tile,), out_shape=(out, out...  16.9 us
    ppermute x3, waiting for transfers between devices, rotated(): lax.ppermute(value, axis, [(i, (i + by) % devices) for i in range(devices)])  7.21 us
    pallas_call x3, Pallas kernels, down_project(): pl.pallas_call(functools.partial(down_kernel, pieces=pieces, first=first,...  4.21 us
    ppermute x3, starting transfers between devices, rotated(): lax.ppermute(value, axis, [(i, (i + by) % devices) for i in range(devices)])  3.87 us
    unnamed x24, local copies, waits for them, and re-layouts  3.57 us
  transfers between devices with their start and end apart: 51, of which 20 were waited for; matrix products, arithmetic and copies ran while one was open for 1% of the time, Pallas kernels for 16%

profile of v1, /device:TPU:0, one launch (start us, length us, event | category | flops | bytes accessed | tf_op | source)
XLA Modules:
  0.0 166.8 jit_solution(3138623666831949636)
XLA Ops:
  2.5 4.1 %collective-permute-start.4 = (bf16[32,2048]{1,0:T(8,128)(2,1)S(1)}, bf16[32,2048]{1,0:T(8,128)(2,1)S(1)}, u32[]{:S(2)}, u32[]{:S(2)}) collective-permute-start(bf16[32,2048]{1,0:T(8,128)(2,1)S(1)} %constant_dynamic-slice_fusion.2.q_ref), channel_id=1, source_target_pairs={{0,8},{4,12},{8,0},{12,4},{1,9},{5,13},{9,1},{13,5},{2,10},{6,14},... | collective-permute-start | bytes 393224 | tf_op jit(solution)/shard_map/ppermute | solution.py:186
  6.5 1.6 collective-permute-start
  8.1 1.9 %copy-done.2 = bf16[3072,512]{1,0:T(8,128)(2,1)S(1)} copy-done((bf16[3072,512]{1,0:T(8,128)(2,1)S(1)}, bf16[3072,512]{1,0:T(8,128)(2,1)}, u32[]{:S(2)}) %copy-start.2) | copy-done | bytes 3145752
  10.3 1.6 copy-done.3
  13.8 6.1 %attend.4 = bf16[528,128]{1,0:T(8,128)(2,1)S(1)} custom-call(s32[4]{0:T(128)S(1)} %get-tuple-element.50.scal_ref, bf16[32,2048]{1,0:T(8,128)(2,1)S(1)} %collective-permute-done.q_ref, bf16[32,256]{1,0:T(8,128)(2,1)S(1)} %get-tuple-element.52.nk_ref, bf16[32,256]{1,0:T(8,128)(2,1)S(1)} %get-tuple-element.53.nv_ref, bf16[3072,512]{1,0:T(8,128)(2,1)S(1)} %load.6.refs_0_, ...), custom_call_target="tpu_custom_call" | custom-call | flops 4831838208 | bytes 12582912 | tf_op jit(solution)/shard_map/attend/pallas_call | solution.py:564
  20.0 6.1 %attend.5 = bf16[528,128]{1,0:T(8,128)(2,1)S(1)} custom-call(s32[4]{0:T(128)S(1)} %get-tuple-element.54.scal_ref, bf16[32,2048]{1,0:T(8,128)(2,1)S(1)} %collective-permute-done.4.q_ref, bf16[32,256]{1,0:T(8,128)(2,1)S(1)} %get-tuple-element.52.nk_ref, bf16[32,256]{1,0:T(8,128)(2,1)S(1)} %get-tuple-element.53.nv_ref, bf16[3072,512]{1,0:T(8,128)(2,1)S(1)} %load.6.refs_0_, ...), custom_call_target="tpu_custom_call" | custom-call | flops 4831838208 | bytes 12582912 | tf_op jit(solution)/shard_map/attend/pallas_call | solution.py:564
  26.1 6.5 %attend.6 = bf16[528,128]{1,0:T(8,128)(2,1)S(1)} custom-call(s32[4]{0:T(128)S(1)} %get-tuple-element.56.scal_ref, bf16[32,2048]{1,0:T(8,128)(2,1)S(1)} %collective-permute-done.6.q_ref, bf16[32,256]{1,0:T(8,128)(2,1)S(1)} %get-tuple-element.52.nk_ref, bf16[32,256]{1,0:T(8,128)(2,1)S(1)} %get-tuple-element.53.nv_ref, bf16[3072,512]{1,0:T(8,128)(2,1)S(1)} %load.6.refs_0_, ...), custom_call_target="tpu_custom_call" | custom-call | flops 4831838208 | bytes 12582912 | tf_op jit(solution)/shard_map/attend/pallas_call | solution.py:564
  32.7 2.9 %collective-permute-start.5 = (bf16[528,128]{1,0:T(8,128)(2,1)S(1)}, bf16[528,128]{1,0:T(8,128)(2,1)S(1)}, u32[]{:S(2)}, u32[]{:S(2)}) collective-permute-start(bf16[528,128]{1,0:T(8,128)(2,1)S(1)} %attend.5), channel_id=1, source_target_pairs={{0,8},{4,12},{8,0},{12,4},{1,9},{5,13},{9,1},{13,5},{2,10},{6,14},... | collective-permute-start | bytes 405512 | tf_op jit(solution)/shard_map/ppermute | solution.py:186
  35.6 1.5 collective-permute-start.3
  37.1 6.1 %attend.7.refs_3_ = bf16[528,128]{1,0:T(8,128)(2,1)S(1)} custom-call(s32[4]{0:T(128)S(1)} %get-tuple-element.58.scal_ref, bf16[32,2048]{1,0:T(8,128)(2,1)S(1)} %constant_dynamic-slice_fusion.2.q_ref, bf16[32,256]{1,0:T(8,128)(2,1)S(1)} %get-tuple-element.52.nk_ref, bf16[32,256]{1,0:T(8,128)(2,1)S(1)} %get-tuple-element.53.nv_ref, ...), custom_call_target="tpu_custom_call" | custom-call | flops 4831838208 | bytes 12582912 | tf_op jit(solution)/shard_map/attend/pallas_call | solution.py:564
  43.3 3.6 %collective-permute-done.5.refs_1_ = bf16[528,128]{1,0:T(8,128)(2,1)S(1)} collective-permute-done((bf16[528,128]{1,0:T(8,128)(2,1)S(1)}, bf16[528,128]{1,0:T(8,128)(2,1)S(1)}, u32[]{:S(2)}, u32[]{:S(2)}) %collective-permute-start.5) | collective-permute-done | bytes 135200 | tf_op jit(solution)/shard_map/ppermute | solution.py:186
  47.3 1.7 %collective-permute-start.9 = (bf16[32,2048]{1,0:T(8,128)(2,1)S(1)}, bf16[32,2048]{1,0:T(8,128)(2,1)S(1)}, u32[]{:S(2)}, u32[]{:S(2)}) collective-permute-start(bf16[32,2048]{1,0:T(8,128)(2,1)S(1)} %merge.1.refs_0_), channel_id=1, source_target_pairs={{0,8},{4,12},{8,0},{12,4},{1,9},{5,13},{9,1},{13,5},{2,10},{6,14},... | collective-permute-start | bytes 393224 | tf_op jit(solution)/shard_map/ppermute | solution.py:181
  49.0 2.1 %collective-permute-start.10 = (bf16[32,2048]{1,0:T(8,128)(2,1)S(1)}, bf16[32,2048]{1,0:T(8,128)(2,1)S(1)}, u32[]{:S(2)}, u32[]{:S(2)}) collective-permute-start(bf16[32,2048]{1,0:T(8,128)(2,1)S(1)} %merge.1.refs_0_), channel_id=1, source_target_pairs={{0,12},{4,0},{8,4},{12,8},{1,13},{5,1},{9,5},{13,9},{2,14},{6,2},{... | collective-permute-start | bytes 393224 | tf_op jit(solution)/shard_map/ppermute | solution.py:181
  51.1 4.3 %collective-permute-done.8.refs_1_ = bf16[32,2048]{1,0:T(8,128)(2,1)S(1)} collective-permute-done((bf16[32,2048]{1,0:T(8,128)(2,1)S(1)}, bf16[32,2048]{1,0:T(8,128)(2,1)S(1)}, u32[]{:S(2)}, u32[]{:S(2)}) %collective-permute-start.8) | collective-permute-done | bytes 131104 | tf_op jit(solution)/shard_map/ppermute | solution.py:181
  55.5 2.9 %collective-permute-done.9.refs_2_ = bf16[32,2048]{1,0:T(8,128)(2,1)S(1)} collective-permute-done((bf16[32,2048]{1,0:T(8,128)(2,1)S(1)}, bf16[32,2048]{1,0:T(8,128)(2,1)S(1)}, u32[]{:S(2)}, u32[]{:S(2)}) %collective-permute-start.9) | collective-permute-done | bytes 131104 | tf_op jit(solution)/shard_map/ppermute | solution.py:181
  59.9 1.3 project.3.refs_1_
  62.2 1.3 project.2.refs_0_
  63.6 1.1 collective-permute-start.15
  64.7 3.0 %collective-permute-done.16.refs_3_ = bf16[128,512]{1,0:T(8,128)(2,1)S(1)} collective-permute-done((bf16[128,512]{1,0:T(8,128)(2,1)S(1)}, bf16[128,512]{1,0:T(8,128)(2,1)S(1)}, u32[]{:S(2)}, u32[]{:S(2)}) %collective-permute-start.16) | collective-permute-done | bytes 131104 | tf_op jit(solution)/shard_map/ppermute | solution.py:186
  67.6 2.2 %collective-permute-done.15.refs_2_ = bf16[128,512]{1,0:T(8,128)(2,1)S(1)} collective-permute-done((bf16[128,512]{1,0:T(8,128)(2,1)S(1)}, bf16[128,512]{1,0:T(8,128)(2,1)S(1)}, u32[]{:S(2)}, u32[]{:S(2)}) %collective-permute-start.15) | collective-permute-done | bytes 131104 | tf_op jit(solution)/shard_map/ppermute | solution.py:186
  70.8 4.8 %gate_up.3 = (bf16[128,2048]{1,0:T(8,128)(2,1)S(1)}, bf16[128,2048]{1,0:T(8,128)(2,1)S(1)}) custom-call(bf16[256,2048]{1,0:T(8,128)(2,1)S(1)} %get-tuple-element.72.left_ref, bf16[1024,2,7168]{2,1,0:T(2,128)(2,1)} %weight_ref.5), custom_call_target="tpu_custom_call" | custom-call | flops 2147483648 | bytes 8388608 | tf_op jit(solution)/shard_map/gate_up/pallas_call | solution.py:647
  75.7 1.9 %collective-permute-done.17.come_ref = bf16[128,2048]{1,0:T(8,128)(2,1)S(1)} collective-permute-done((bf16[128,2048]{1,0:T(8,128)(2,1)S(1)}, bf16[128,2048]{1,0:T(8,128)(2,1)S(1)}, u32[]{:S(2)}, u32[]{:S(2)}) %collective-permute-start.17) | collective-permute-done | bytes 524320 | tf_op jit(solution)/shard_map/ppermute | solution.py:186
  77.8 7.1 %gate_up.4 = (bf16[128,3072]{1,0:T(8,128)(2,1)S(1)}, bf16[128,3072]{1,0:T(8,128)(2,1)S(1)}) custom-call(bf16[256,2048]{1,0:T(8,128)(2,1)S(1)} %get-tuple-element.72.left_ref, bf16[1024,2,7168]{2,1,0:T(2,128)(2,1)} %weight_ref.5), custom_call_target="tpu_custom_call" | custom-call | flops 3221225472 | bytes 12582912 | tf_op jit(solution)/shard_map/gate_up/pallas_call | solution.py:647
  85.1 2.2 %collective-permute-done.18.come_ref = bf16[128,3072]{1,0:T(8,128)(2,1)S(1)} collective-permute-done((bf16[128,3072]{1,0:T(8,128)(2,1)S(1)}, bf16[128,3072]{1,0:T(8,128)(2,1)S(1)}, u32[]{:S(2)}, u32[]{:S(2)}) %collective-permute-start.18) | collective-permute-done | bytes 786464 | tf_op jit(solution)/shard_map/ppermute | solution.py:186
  87.5 5.0 %gate_up.5 = (bf16[128,2048]{1,0:T(8,128)(2,1)S(1)}, bf16[128,2048]{1,0:T(8,128)(2,1)S(1)}) custom-call(bf16[256,2048]{1,0:T(8,128)(2,1)S(1)} %get-tuple-element.72.left_ref, bf16[1024,2,7168]{2,1,0:T(2,128)(2,1)} %weight_ref.5), custom_call_target="tpu_custom_call" | custom-call | flops 2147483648 | bytes 8388608 | tf_op jit(solution)/shard_map/gate_up/pallas_call | solution.py:647
  92.7 2.0 %collective-permute-start.32 = (bf16[128,1536]{1,0:T(8,128)(2,1)S(1)}, bf16[128,1536]{1,0:T(8,128)(2,1)S(1)}, u32[]{:S(2)}, u32[]{:S(2)}) collective-permute-start(bf16[128,1536]{1,0:T(8,128)(2,1)S(1)} %get-tuple-element.82), channel_id=1, source_target_pairs={{0,4},{4,0},{8,12},{12,8},{1,5},{5,1},{9,13},{13,9},{2,6},{6,2},{1... | collective-permute-start | bytes 1179656 | tf_op jit(solution)/shard_map/ppermute | solution.py:186
  94.9 2.1 %collective-permute-start.20 = (bf16[128,1024]{1,0:T(8,128)(2,1)S(1)}, bf16[128,1024]{1,0:T(8,128)(2,1)S(1)}, u32[]{:S(2)}, u32[]{:S(2)}) collective-permute-start(bf16[128,1024]{1,0:T(8,128)(2,1)S(1)} %get-tuple-element.77), channel_id=1, source_target_pairs={{0,4},{4,0},{8,12},{12,8},{1,5},{5,1},{9,13},{13,9},{2,6},{6,2},{1... | collective-permute-start | bytes 786440 | tf_op jit(solution)/shard_map/ppermute | solution.py:186
  96.9 7.7 %collective-permute-done.32.come_ref = bf16[128,1536]{1,0:T(8,128)(2,1)S(1)} collective-permute-done((bf16[128,1536]{1,0:T(8,128)(2,1)S(1)}, bf16[128,1536]{1,0:T(8,128)(2,1)S(1)}, u32[]{:S(2)}, u32[]{:S(2)}) %collective-permute-start.32) | collective-permute-done | bytes 393248 | tf_op jit(solution)/shard_map/ppermute | solution.py:186
  104.8 1.4 collective-permute-start.33
  106.2 8.3 %collective-permute-done.41.come_ref = bf16[128,1024]{1,0:T(8,128)(2,1)S(1)} collective-permute-done((bf16[128,1024]{1,0:T(8,128)(2,1)S(1)}, bf16[128,1024]{1,0:T(8,128)(2,1)S(1)}, u32[]{:S(2)}, u32[]{:S(2)}) %collective-permute-start.41) | collective-permute-done | bytes 262176 | tf_op jit(solution)/shard_map/ppermute | solution.py:186
  115.5 2.5 %collective-permute-start.22 = (f32[8,128]{1,0:T(8,128)S(1)}, f32[8,128]{1,0:T(8,128)S(1)}, u32[]{:S(2)}, u32[]{:S(2)}) collective-permute-start(f32[8,128]{1,0:T(8,128)S(1)} %get-tuple-element.80), channel_id=1, source_target_pairs={{0,4},{4,0},{8,12},{12,8},{1,5},{5,1},{9,13},{13,9},{2,6},{6,2},{1... | collective-permute-start | bytes 12296 | tf_op jit(solution)/shard_map/ppermute | solution.py:186
  118.0 4.0 %collective-permute-done.22 = f32[8,128]{1,0:T(8,128)S(1)} collective-permute-done((f32[8,128]{1,0:T(8,128)S(1)}, f32[8,128]{1,0:T(8,128)S(1)}, u32[]{:S(2)}, u32[]{:S(2)}) %collective-permute-start.22) | collective-permute-done | bytes 4128 | tf_op jit(solution)/shard_map/ppermute | solution.py:186
  122.0 2.1 %collective-permute-start.23 = (f32[8,128]{1,0:T(8,128)S(1)}, f32[8,128]{1,0:T(8,128)S(1)}, u32[]{:S(2)}, u32[]{:S(2)}) collective-permute-start(f32[8,128]{1,0:T(8,128)S(1)} %add.114), channel_id=1, source_target_pairs={{0,8},{4,12},{8,0},{12,4},{1,9},{5,13},{9,1},{13,5},{2,10},{6,14},... | collective-permute-start | bytes 12296 | tf_op jit(solution)/shard_map/ppermute | solution.py:186
  124.1 2.4 %collective-permute-done.23 = f32[8,128]{1,0:T(8,128)S(1)} collective-permute-done((f32[8,128]{1,0:T(8,128)S(1)}, f32[8,128]{1,0:T(8,128)S(1)}, u32[]{:S(2)}, u32[]{:S(2)}) %collective-permute-start.23) | collective-permute-done | bytes 4128 | tf_op jit(solution)/shard_map/ppermute | solution.py:186
  126.5 1.2 collective-permute-done.24
  128.4 2.1 %collective-permute-start.44 = (bf16[64,512]{1,0:T(8,128)(2,1)S(1)}, bf16[64,512]{1,0:T(8,128)(2,1)S(1)}, u32[]{:S(2)}, u32[]{:S(2)}) collective-permute-start(bf16[64,512]{1,0:T(8,128)(2,1)S(1)} %activate.5.refs_0_), channel_id=1, source_target_pairs={{0,8},{4,12},{8,0},{12,4},{1,9},{5,13},{9,1},{13,5},{2,10},{6,14},... | collective-permute-start | bytes 196616 | tf_op jit(solution)/shard_map/ppermute | solution.py:186
  130.5 1.1 collective-permute-start.43
  131.7 2.3 %collective-permute-start.21 = (bf16[128,512]{1,0:T(8,128)(2,1)S(1)}, bf16[128,512]{1,0:T(8,128)(2,1)S(1)}, u32[]{:S(2)}, u32[]{:S(2)}) collective-permute-start(bf16[128,512]{1,0:T(8,128)(2,1)S(1)} %get-tuple-element.79), channel_id=1, source_target_pairs={{0,8},{4,12},{8,0},{12,4},{1,9},{5,13},{9,1},{13,5},{2,10},{6,14},... | collective-permute-start | bytes 393224 | tf_op jit(solution)/shard_map/ppermute | solution.py:186
  135.5 1.5 collective-permute-start.45
  137.7 3.4 %collective-permute-done.45.refs_3_ = bf16[64,512]{1,0:T(8,128)(2,1)S(1)} collective-permute-done((bf16[64,512]{1,0:T(8,128)(2,1)S(1)}, bf16[64,512]{1,0:T(8,128)(2,1)S(1)}, u32[]{:S(2)}, u32[]{:S(2)}) %collective-permute-start.45) | collective-permute-done | bytes 65568 | tf_op jit(solution)/shard_map/ppermute | solution.py:186
  141.1 4.3 %collective-permute-done.35.refs_2_ = bf16[64,768]{1,0:T(8,128)(2,1)S(1)} collective-permute-done((bf16[64,768]{1,0:T(8,128)(2,1)S(1)}, bf16[64,768]{1,0:T(8,128)(2,1)S(1)}, u32[]{:S(2)}, u32[]{:S(2)}) %collective-permute-start.35) | collective-permute-done | bytes 98336 | tf_op jit(solution)/shard_map/ppermute | solution.py:186
  146.7 2.6 %collective-permute-start.26 = (bf16[64,512]{1,0:T(8,128)(2,1)S(1)}, bf16[64,512]{1,0:T(8,128)(2,1)S(1)}, u32[]{:S(2)}, u32[]{:S(2)}) collective-permute-start(bf16[64,512]{1,0:T(8,128)(2,1)S(1)} %activate.3.refs_0_), channel_id=1, source_target_pairs={{0,8},{4,12},{8,0},{12,4},{1,9},{5,13},{9,1},{13,5},{2,10},{6,14},... | collective-permute-start | bytes 196616 | tf_op jit(solution)/shard_map/ppermute | solution.py:186
  150.1 2.5 %collective-permute-done.26.refs_2_ = bf16[64,512]{1,0:T(8,128)(2,1)S(1)} collective-permute-done((bf16[64,512]{1,0:T(8,128)(2,1)S(1)}, bf16[64,512]{1,0:T(8,128)(2,1)S(1)}, u32[]{:S(2)}, u32[]{:S(2)}) %collective-permute-start.26) | collective-permute-done | bytes 65568 | tf_op jit(solution)/shard_map/ppermute | solution.py:186
  152.6 1.3 collective-permute-start.27
  155.1 1.3 down.3.refs_8_
  157.5 1.6 down.4.refs_8_
  159.1 1.4 down.5
  161.6 4.5 %collective-permute-done.50 = bf16[64,1024]{1,0:T(8,128)(2,1)S(1)} collective-permute-done((bf16[64,1024]{1,0:T(8,128)(2,1)S(1)}, bf16[64,1024]{1,0:T(8,128)(2,1)S(1)}, u32[]{:S(2)}, u32[]{:S(2)}) %collective-permute-start.50) | collective-permute-done | bytes 131104 | tf_op jit(solution)/shard_map/ppermute | solution.py:186
  (120 shorter events, 19.0 us)
Async XLA Ops:
  0.0 13.8 %collective-permute-start.1 = (bf16[3072,512]{1,0:T(8,128)(2,1)}, bf16[3072,512]{1,0:T(8,128)(2,1)}, u32[]{:S(2)}, u32[]{:S(2)}) collective-permute-start(bf16[3072,512]{1,0:T(8,128)(2,1)} %source_ref.6), channel_id=1, source_target_pairs={{0,1},{1,0},{2,3},{3,2},{4,5},{5,4},{6,7},{7,6},{8,9},{9,8},{10,11... | collective-permute-start | bytes 9437192 | tf_op jit(solution)/shard_map/ppermute | solution.py:186
  0.5 13.3 %collective-permute-start.2 = (bf16[3072,512]{1,0:T(8,128)(2,1)}, bf16[3072,512]{1,0:T(8,128)(2,1)}, u32[]{:S(2)}, u32[]{:S(2)}) collective-permute-start(bf16[3072,512]{1,0:T(8,128)(2,1)} %source_ref.7), channel_id=1, source_target_pairs={{0,1},{1,0},{2,3},{3,2},{4,5},{5,4},{6,7},{7,6},{8,9},{9,8},{10,11... | collective-permute-start | bytes 9437192 | tf_op jit(solution)/shard_map/ppermute | solution.py:186
  2.5 10.7 %collective-permute-start.4 = (bf16[32,2048]{1,0:T(8,128)(2,1)S(1)}, bf16[32,2048]{1,0:T(8,128)(2,1)S(1)}, u32[]{:S(2)}, u32[]{:S(2)}) collective-permute-start(bf16[32,2048]{1,0:T(8,128)(2,1)S(1)} %constant_dynamic-slice_fusion.2.q_ref), channel_id=1, source_target_pairs={{0,8},{4,12},{8,0},{12,4},{1,9},{5,13},{9,1},{13,5},{2,10},{6,14},... | collective-permute-start | bytes 393224 | tf_op jit(solution)/shard_map/ppermute | solution.py:186
  6.5 7.3 %collective-permute-start = (bf16[32,2048]{1,0:T(8,128)(2,1)S(1)}, bf16[32,2048]{1,0:T(8,128)(2,1)S(1)}, u32[]{:S(2)}, u32[]{:S(2)}) collective-permute-start(bf16[32,2048]{1,0:T(8,128)(2,1)S(1)} %constant_dynamic-slice_fusion.2.q_ref), channel_id=1, source_target_pairs={{0,4},{4,0},{8,12},{12,8},{1,5},{5,1},{9,13},{13,9},{2,6},{6,2},{1... | collective-permute-start | bytes 393224 | tf_op jit(solution)/shard_map/ppermute | solution.py:186
  13.2 12.9 %collective-permute-start.6 = (bf16[32,2048]{1,0:T(8,128)(2,1)S(1)}, bf16[32,2048]{1,0:T(8,128)(2,1)S(1)}, u32[]{:S(2)}, u32[]{:S(2)}) collective-permute-start(bf16[32,2048]{1,0:T(8,128)(2,1)S(1)} %collective-permute-done.4.q_ref), channel_id=1, source_target_pairs={{0,4},{4,0},{8,12},{12,8},{1,5},{5,1},{9,13},{13,9},{2,6},{6,2},{1... | collective-permute-start | bytes 393224 | tf_op jit(solution)/shard_map/ppermute | solution.py:186
  32.6 10.6 %collective-permute-start.7 = (bf16[528,128]{1,0:T(8,128)(2,1)S(1)}, bf16[528,128]{1,0:T(8,128)(2,1)S(1)}, u32[]{:S(2)}, u32[]{:S(2)}) collective-permute-start(bf16[528,128]{1,0:T(8,128)(2,1)S(1)} %attend.6), channel_id=1, source_target_pairs={{0,12},{4,8},{8,4},{12,0},{1,13},{5,9},{9,5},{13,1},{2,14},{6,10},... | collective-permute-start | bytes 405512 | tf_op jit(solution)/shard_map/ppermute | solution.py:186
  32.7 14.1 %collective-permute-start.5 = (bf16[528,128]{1,0:T(8,128)(2,1)S(1)}, bf16[528,128]{1,0:T(8,128)(2,1)S(1)}, u32[]{:S(2)}, u32[]{:S(2)}) collective-permute-start(bf16[528,128]{1,0:T(8,128)(2,1)S(1)} %attend.5), channel_id=1, source_target_pairs={{0,8},{4,12},{8,0},{12,4},{1,9},{5,13},{9,1},{13,5},{2,10},{6,14},... | collective-permute-start | bytes 405512 | tf_op jit(solution)/shard_map/ppermute | solution.py:186
  35.6 11.2 %collective-permute-start.3 = (bf16[528,128]{1,0:T(8,128)(2,1)S(1)}, bf16[528,128]{1,0:T(8,128)(2,1)S(1)}, u32[]{:S(2)}, u32[]{:S(2)}) collective-permute-start(bf16[528,128]{1,0:T(8,128)(2,1)S(1)} %attend.4), channel_id=1, source_target_pairs={{0,4},{4,0},{8,12},{12,8},{1,5},{5,1},{9,13},{13,9},{2,6},{6,2},{1... | collective-permute-start | bytes 405512 | tf_op jit(solution)/shard_map/ppermute | solution.py:186
  47.2 8.2 %collective-permute-start.8 = (bf16[32,2048]{1,0:T(8,128)(2,1)S(1)}, bf16[32,2048]{1,0:T(8,128)(2,1)S(1)}, u32[]{:S(2)}, u32[]{:S(2)}) collective-permute-start(bf16[32,2048]{1,0:T(8,128)(2,1)S(1)} %merge.1.refs_0_), channel_id=1, source_target_pairs={{0,4},{4,8},{8,12},{12,0},{1,5},{5,9},{9,13},{13,1},{2,6},{6,10},{... | collective-permute-start | bytes 393224 | tf_op jit(solution)/shard_map/ppermute | solution.py:181
  47.3 11.0 %collective-permute-start.9 = (bf16[32,2048]{1,0:T(8,128)(2,1)S(1)}, bf16[32,2048]{1,0:T(8,128)(2,1)S(1)}, u32[]{:S(2)}, u32[]{:S(2)}) collective-permute-start(bf16[32,2048]{1,0:T(8,128)(2,1)S(1)} %merge.1.refs_0_), channel_id=1, source_target_pairs={{0,8},{4,12},{8,0},{12,4},{1,9},{5,13},{9,1},{13,5},{2,10},{6,14},... | collective-permute-start | bytes 393224 | tf_op jit(solution)/shard_map/ppermute | solution.py:181
  49.0 9.3 %collective-permute-start.10 = (bf16[32,2048]{1,0:T(8,128)(2,1)S(1)}, bf16[32,2048]{1,0:T(8,128)(2,1)S(1)}, u32[]{:S(2)}, u32[]{:S(2)}) collective-permute-start(bf16[32,2048]{1,0:T(8,128)(2,1)S(1)} %merge.1.refs_0_), channel_id=1, source_target_pairs={{0,12},{4,0},{8,4},{12,8},{1,13},{5,1},{9,5},{13,9},{2,14},{6,2},{... | collective-permute-start | bytes 393224 | tf_op jit(solution)/shard_map/ppermute | solution.py:181
  51.1 8.3 %collective-permute-start.11 = (bf16[32,2048]{1,0:T(8,128)(2,1)S(1)}, bf16[32,2048]{1,0:T(8,128)(2,1)S(1)}, u32[]{:S(2)}, u32[]{:S(2)}) collective-permute-start(bf16[32,2048]{1,0:T(8,128)(2,1)S(1)} %merge.1.refs_0_), channel_id=1, source_target_pairs={{0,1},{1,0},{2,3},{3,2},{4,5},{5,4},{6,7},{7,6},{8,9},{9,8},{10,11... | collective-permute-start | bytes 393224 | tf_op jit(solution)/shard_map/ppermute | solution.py:186
  55.5 4.0 %collective-permute-start.12 = (bf16[32,2048]{1,0:T(8,128)(2,1)S(1)}, bf16[32,2048]{1,0:T(8,128)(2,1)S(1)}, u32[]{:S(2)}, u32[]{:S(2)}) collective-permute-start(bf16[32,2048]{1,0:T(8,128)(2,1)S(1)} %collective-permute-done.8.refs_1_), channel_id=1, source_target_pairs={{0,1},{1,0},{2,3},{3,2},{4,5},{5,4},{6,7},{7,6},{8,9},{9,8},{10,11... | collective-permute-start | bytes 393224 | tf_op jit(solution)/shard_map/ppermute | solution.py:186
  58.3 1.5 collective-permute-start.14
  61.2 6.4 %collective-permute-start.16 = (bf16[128,512]{1,0:T(8,128)(2,1)S(1)}, bf16[128,512]{1,0:T(8,128)(2,1)S(1)}, u32[]{:S(2)}, u32[]{:S(2)}) collective-permute-start(bf16[128,512]{1,0:T(8,128)(2,1)S(1)} %project.3.refs_1_), channel_id=1, source_target_pairs={{0,2},{2,0},{1,3},{3,1},{4,6},{6,4},{5,7},{7,5},{8,10},{10,8},{9,1... | collective-permute-start | bytes 393224 | tf_op jit(solution)/shard_map/ppermute | solution.py:186
  63.6 6.2 %collective-permute-start.15 = (bf16[128,512]{1,0:T(8,128)(2,1)S(1)}, bf16[128,512]{1,0:T(8,128)(2,1)S(1)}, u32[]{:S(2)}, u32[]{:S(2)}) collective-permute-start(bf16[128,512]{1,0:T(8,128)(2,1)S(1)} %project.2.refs_0_), channel_id=1, source_target_pairs={{0,2},{2,0},{1,3},{3,1},{4,6},{6,4},{5,7},{7,5},{8,10},{10,8},{9,1... | collective-permute-start | bytes 393224 | tf_op jit(solution)/shard_map/ppermute | solution.py:186
  75.6 2.0 %collective-permute-start.17 = (bf16[128,2048]{1,0:T(8,128)(2,1)S(1)}, bf16[128,2048]{1,0:T(8,128)(2,1)S(1)}, u32[]{:S(2)}, u32[]{:S(2)}) collective-permute-start(bf16[128,2048]{1,0:T(8,128)(2,1)S(1)} %get-tuple-element.66), channel_id=1, source_target_pairs={{0,1},{1,0},{2,3},{3,2},{4,5},{5,4},{6,7},{7,6},{8,9},{9,8},{10,11... | collective-permute-start | bytes 1572872 | tf_op jit(solution)/shard_map/ppermute | solution.py:186
  84.9 2.4 %collective-permute-start.18 = (bf16[128,3072]{1,0:T(8,128)(2,1)S(1)}, bf16[128,3072]{1,0:T(8,128)(2,1)S(1)}, u32[]{:S(2)}, u32[]{:S(2)}) collective-permute-start(bf16[128,3072]{1,0:T(8,128)(2,1)S(1)} %get-tuple-element.70), channel_id=1, source_target_pairs={{0,1},{1,0},{2,3},{3,2},{4,5},{5,4},{6,7},{7,6},{8,9},{9,8},{10,11... | collective-permute-start | bytes 2359304 | tf_op jit(solution)/shard_map/ppermute | solution.py:186
  92.5 2.3 %collective-permute-start.19 = (bf16[128,2048]{1,0:T(8,128)(2,1)S(1)}, bf16[128,2048]{1,0:T(8,128)(2,1)S(1)}, u32[]{:S(2)}, u32[]{:S(2)}) collective-permute-start(bf16[128,2048]{1,0:T(8,128)(2,1)S(1)} %get-tuple-element.74), channel_id=1, source_target_pairs={{0,1},{1,0},{2,3},{3,2},{4,5},{5,4},{6,7},{7,6},{8,9},{9,8},{10,11... | collective-permute-start | bytes 1572872 | tf_op jit(solution)/shard_map/ppermute | solution.py:186
  92.7 12.0 %collective-permute-start.32 = (bf16[128,1536]{1,0:T(8,128)(2,1)S(1)}, bf16[128,1536]{1,0:T(8,128)(2,1)S(1)}, u32[]{:S(2)}, u32[]{:S(2)}) collective-permute-start(bf16[128,1536]{1,0:T(8,128)(2,1)S(1)} %get-tuple-element.82), channel_id=1, source_target_pairs={{0,4},{4,0},{8,12},{12,8},{1,5},{5,1},{9,13},{13,9},{2,6},{6,2},{1... | collective-permute-start | bytes 1179656 | tf_op jit(solution)/shard_map/ppermute | solution.py:186
  94.7 19.8 %collective-permute-start.41 = (bf16[128,1024]{1,0:T(8,128)(2,1)S(1)}, bf16[128,1024]{1,0:T(8,128)(2,1)S(1)}, u32[]{:S(2)}, u32[]{:S(2)}) collective-permute-start(bf16[128,1024]{1,0:T(8,128)(2,1)S(1)} %get-tuple-element.86), channel_id=1, source_target_pairs={{0,4},{4,0},{8,12},{12,8},{1,5},{5,1},{9,13},{13,9},{2,6},{6,2},{1... | collective-permute-start | bytes 786440 | tf_op jit(solution)/shard_map/ppermute | solution.py:186
  94.9 36.7 %collective-permute-start.20 = (bf16[128,1024]{1,0:T(8,128)(2,1)S(1)}, bf16[128,1024]{1,0:T(8,128)(2,1)S(1)}, u32[]{:S(2)}, u32[]{:S(2)}) collective-permute-start(bf16[128,1024]{1,0:T(8,128)(2,1)S(1)} %get-tuple-element.77), channel_id=1, source_target_pairs={{0,4},{4,0},{8,12},{12,8},{1,5},{5,1},{9,13},{13,9},{2,6},{6,2},{1... | collective-permute-start | bytes 786440 | tf_op jit(solution)/shard_map/ppermute | solution.py:186
  104.8 29.2 %collective-permute-start.33 = (bf16[128,768]{1,0:T(8,128)(2,1)S(1)}, bf16[128,768]{1,0:T(8,128)(2,1)S(1)}, u32[]{:S(2)}, u32[]{:S(2)}) collective-permute-start(bf16[128,768]{1,0:T(8,128)(2,1)S(1)} %get-tuple-element.84), channel_id=1, source_target_pairs={{0,8},{4,12},{8,0},{12,4},{1,9},{5,13},{9,1},{13,5},{2,10},{6,14},... | collective-permute-start | bytes 589832 | tf_op jit(solution)/shard_map/ppermute | solution.py:186
  114.6 13.1 %collective-permute-start.42 = (bf16[128,512]{1,0:T(8,128)(2,1)S(1)}, bf16[128,512]{1,0:T(8,128)(2,1)S(1)}, u32[]{:S(2)}, u32[]{:S(2)}) collective-permute-start(bf16[128,512]{1,0:T(8,128)(2,1)S(1)} %get-tuple-element.88), channel_id=1, source_target_pairs={{0,8},{4,12},{8,0},{12,4},{1,9},{5,13},{9,1},{13,5},{2,10},{6,14},... | collective-permute-start | bytes 393224 | tf_op jit(solution)/shard_map/ppermute | solution.py:186
  115.5 6.5 %collective-permute-start.22 = (f32[8,128]{1,0:T(8,128)S(1)}, f32[8,128]{1,0:T(8,128)S(1)}, u32[]{:S(2)}, u32[]{:S(2)}) collective-permute-start(f32[8,128]{1,0:T(8,128)S(1)} %get-tuple-element.80), channel_id=1, source_target_pairs={{0,4},{4,0},{8,12},{12,8},{1,5},{5,1},{9,13},{13,9},{2,6},{6,2},{1... | collective-permute-start | bytes 12296 | tf_op jit(solution)/shard_map/ppermute | solution.py:186
  122.0 4.5 %collective-permute-start.23 = (f32[8,128]{1,0:T(8,128)S(1)}, f32[8,128]{1,0:T(8,128)S(1)}, u32[]{:S(2)}, u32[]{:S(2)}) collective-permute-start(f32[8,128]{1,0:T(8,128)S(1)} %add.114), channel_id=1, source_target_pairs={{0,8},{4,12},{8,0},{12,4},{1,9},{5,13},{9,1},{13,5},{2,10},{6,14},... | collective-permute-start | bytes 12296 | tf_op jit(solution)/shard_map/ppermute | solution.py:186
  128.4 7.1 %collective-permute-start.44 = (bf16[64,512]{1,0:T(8,128)(2,1)S(1)}, bf16[64,512]{1,0:T(8,128)(2,1)S(1)}, u32[]{:S(2)}, u32[]{:S(2)}) collective-permute-start(bf16[64,512]{1,0:T(8,128)(2,1)S(1)} %activate.5.refs_0_), channel_id=1, source_target_pairs={{0,8},{4,12},{8,0},{12,4},{1,9},{5,13},{9,1},{13,5},{2,10},{6,14},... | collective-permute-start | bytes 196616 | tf_op jit(solution)/shard_map/ppermute | solution.py:186
  130.5 6.4 %collective-permute-start.43 = (bf16[64,512]{1,0:T(8,128)(2,1)S(1)}, bf16[64,512]{1,0:T(8,128)(2,1)S(1)}, u32[]{:S(2)}, u32[]{:S(2)}) collective-permute-start(bf16[64,512]{1,0:T(8,128)(2,1)S(1)} %activate.5.refs_0_), channel_id=1, source_target_pairs={{0,4},{4,0},{8,12},{12,8},{1,5},{5,1},{9,13},{13,9},{2,6},{6,2},{1... | collective-permute-start | bytes 196616 | tf_op jit(solution)/shard_map/ppermute | solution.py:186
  131.7 13.8 %collective-permute-start.21 = (bf16[128,512]{1,0:T(8,128)(2,1)S(1)}, bf16[128,512]{1,0:T(8,128)(2,1)S(1)}, u32[]{:S(2)}, u32[]{:S(2)}) collective-permute-start(bf16[128,512]{1,0:T(8,128)(2,1)S(1)} %get-tuple-element.79), channel_id=1, source_target_pairs={{0,8},{4,12},{8,0},{12,4},{1,9},{5,13},{9,1},{13,5},{2,10},{6,14},... | collective-permute-start | bytes 393224 | tf_op jit(solution)/shard_map/ppermute | solution.py:186
  134.7 10.8 %collective-permute-start.35 = (bf16[64,768]{1,0:T(8,128)(2,1)S(1)}, bf16[64,768]{1,0:T(8,128)(2,1)S(1)}, u32[]{:S(2)}, u32[]{:S(2)}) collective-permute-start(bf16[64,768]{1,0:T(8,128)(2,1)S(1)} %activate.4.refs_0_), channel_id=1, source_target_pairs={{0,8},{4,12},{8,0},{12,4},{1,9},{5,13},{9,1},{13,5},{2,10},{6,14},... | collective-permute-start | bytes 294920 | tf_op jit(solution)/shard_map/ppermute | solution.py:186
  135.5 5.7 %collective-permute-start.45 = (bf16[64,512]{1,0:T(8,128)(2,1)S(1)}, bf16[64,512]{1,0:T(8,128)(2,1)S(1)}, u32[]{:S(2)}, u32[]{:S(2)}) collective-permute-start(bf16[64,512]{1,0:T(8,128)(2,1)S(1)} %collective-permute-done.44.refs_2_), channel_id=1, source_target_pairs={{0,4},{4,0},{8,12},{12,8},{1,5},{5,1},{9,13},{13,9},{2,6},{6,2},{1... | collective-permute-start | bytes 196616 | tf_op jit(solution)/shard_map/ppermute | solution.py:186
  136.9 8.6 %collective-permute-start.47 = (bf16[64,512]{1,0:T(8,128)(2,1)S(1)}, bf16[64,512]{1,0:T(8,128)(2,1)S(1)}, u32[]{:S(2)}, u32[]{:S(2)}) collective-permute-start(bf16[64,512]{1,0:T(8,128)(2,1)S(1)} %collective-permute-done.43.refs_1_), channel_id=1, source_target_pairs={{0,1},{1,0},{2,3},{3,2},{4,5},{5,4},{6,7},{7,6},{8,9},{9,8},{10,11... | collective-permute-start | bytes 196616 | tf_op jit(solution)/shard_map/ppermute | solution.py:186
  136.9 12.4 %collective-permute-start.34 = (bf16[64,768]{1,0:T(8,128)(2,1)S(1)}, bf16[64,768]{1,0:T(8,128)(2,1)S(1)}, u32[]{:S(2)}, u32[]{:S(2)}) collective-permute-start(bf16[64,768]{1,0:T(8,128)(2,1)S(1)} %activate.4.refs_0_), channel_id=1, source_target_pairs={{0,4},{4,0},{8,12},{12,8},{1,5},{5,1},{9,13},{13,9},{2,6},{6,2},{1... | collective-permute-start | bytes 294920 | tf_op jit(solution)/shard_map/ppermute | solution.py:186
  141.1 5.5 %collective-permute-start.48 = (bf16[64,512]{1,0:T(8,128)(2,1)S(1)}, bf16[64,512]{1,0:T(8,128)(2,1)S(1)}, u32[]{:S(2)}, u32[]{:S(2)}) collective-permute-start(bf16[64,512]{1,0:T(8,128)(2,1)S(1)} %collective-permute-done.44.refs_2_), channel_id=1, source_target_pairs={{0,1},{1,0},{2,3},{3,2},{4,5},{5,4},{6,7},{7,6},{8,9},{9,8},{10,11... | collective-permute-start | bytes 196616 | tf_op jit(solution)/shard_map/ppermute | solution.py:186
  145.5 4.6 %collective-permute-start.36 = (bf16[64,768]{1,0:T(8,128)(2,1)S(1)}, bf16[64,768]{1,0:T(8,128)(2,1)S(1)}, u32[]{:S(2)}, u32[]{:S(2)}) collective-permute-start(bf16[64,768]{1,0:T(8,128)(2,1)S(1)} %collective-permute-done.35.refs_2_), channel_id=1, source_target_pairs={{0,4},{4,0},{8,12},{12,8},{1,5},{5,1},{9,13},{13,9},{2,6},{6,2},{1... | collective-permute-start | bytes 294920 | tf_op jit(solution)/shard_map/ppermute | solution.py:186
  145.5 3.8 %collective-permute-start.49 = (bf16[64,512]{1,0:T(8,128)(2,1)S(1)}, bf16[64,512]{1,0:T(8,128)(2,1)S(1)}, u32[]{:S(2)}, u32[]{:S(2)}) collective-permute-start(bf16[64,512]{1,0:T(8,128)(2,1)S(1)} %collective-permute-done.45.refs_3_), channel_id=1, source_target_pairs={{0,1},{1,0},{2,3},{3,2},{4,5},{5,4},{6,7},{7,6},{8,9},{9,8},{10,11... | collective-permute-start | bytes 196616 | tf_op jit(solution)/shard_map/ppermute | solution.py:186
  145.5 4.6 %collective-permute-start.37 = (bf16[64,768]{1,0:T(8,128)(2,1)S(1)}, bf16[64,768]{1,0:T(8,128)(2,1)S(1)}, u32[]{:S(2)}, u32[]{:S(2)}) collective-permute-start(bf16[64,768]{1,0:T(8,128)(2,1)S(1)} %activate.4.refs_0_), channel_id=1, source_target_pairs={{0,1},{1,0},{2,3},{3,2},{4,5},{5,4},{6,7},{7,6},{8,9},{9,8},{10,11... | collective-permute-start | bytes 294920 | tf_op jit(solution)/shard_map/ppermute | solution.py:186
  146.7 5.9 %collective-permute-start.26 = (bf16[64,512]{1,0:T(8,128)(2,1)S(1)}, bf16[64,512]{1,0:T(8,128)(2,1)S(1)}, u32[]{:S(2)}, u32[]{:S(2)}) collective-permute-start(bf16[64,512]{1,0:T(8,128)(2,1)S(1)} %activate.3.refs_0_), channel_id=1, source_target_pairs={{0,8},{4,12},{8,0},{12,4},{1,9},{5,13},{9,1},{13,5},{2,10},{6,14},... | collective-permute-start | bytes 196616 | tf_op jit(solution)/shard_map/ppermute | solution.py:186
  149.3 7.1 %collective-permute-start.38 = (bf16[64,768]{1,0:T(8,128)(2,1)S(1)}, bf16[64,768]{1,0:T(8,128)(2,1)S(1)}, u32[]{:S(2)}, u32[]{:S(2)}) collective-permute-start(bf16[64,768]{1,0:T(8,128)(2,1)S(1)} %collective-permute-done.34.refs_1_), channel_id=1, source_target_pairs={{0,1},{1,0},{2,3},{3,2},{4,5},{5,4},{6,7},{7,6},{8,9},{9,8},{10,11... | collective-permute-start | bytes 294920 | tf_op jit(solution)/shard_map/ppermute | solution.py:186
  149.3 7.2 %collective-permute-start.39 = (bf16[64,768]{1,0:T(8,128)(2,1)S(1)}, bf16[64,768]{1,0:T(8,128)(2,1)S(1)}, u32[]{:S(2)}, u32[]{:S(2)}) collective-permute-start(bf16[64,768]{1,0:T(8,128)(2,1)S(1)} %collective-permute-done.35.refs_2_), channel_id=1, source_target_pairs={{0,1},{1,0},{2,3},{3,2},{4,5},{5,4},{6,7},{7,6},{8,9},{9,8},{10,11... | collective-permute-start | bytes 294920 | tf_op jit(solution)/shard_map/ppermute | solution.py:186
  150.1 7.4 %collective-permute-start.40 = (bf16[64,768]{1,0:T(8,128)(2,1)S(1)}, bf16[64,768]{1,0:T(8,128)(2,1)S(1)}, u32[]{:S(2)}, u32[]{:S(2)}) collective-permute-start(bf16[64,768]{1,0:T(8,128)(2,1)S(1)} %collective-permute-done.36.refs_3_), channel_id=1, source_target_pairs={{0,1},{1,0},{2,3},{3,2},{4,5},{5,4},{6,7},{7,6},{8,9},{9,8},{10,11... | collective-permute-start | bytes 294920 | tf_op jit(solution)/shard_map/ppermute | solution.py:186
  150.1 6.9 %collective-permute-start.25 = (bf16[64,512]{1,0:T(8,128)(2,1)S(1)}, bf16[64,512]{1,0:T(8,128)(2,1)S(1)}, u32[]{:S(2)}, u32[]{:S(2)}) collective-permute-start(bf16[64,512]{1,0:T(8,128)(2,1)S(1)} %activate.3.refs_0_), channel_id=1, source_target_pairs={{0,4},{4,0},{8,12},{12,8},{1,5},{5,1},{9,13},{13,9},{2,6},{6,2},{1... | collective-permute-start | bytes 196616 | tf_op jit(solution)/shard_map/ppermute | solution.py:186
  152.6 4.5 %collective-permute-start.27 = (bf16[64,512]{1,0:T(8,128)(2,1)S(1)}, bf16[64,512]{1,0:T(8,128)(2,1)S(1)}, u32[]{:S(2)}, u32[]{:S(2)}) collective-permute-start(bf16[64,512]{1,0:T(8,128)(2,1)S(1)} %collective-permute-done.26.refs_2_), channel_id=1, source_target_pairs={{0,4},{4,0},{8,12},{12,8},{1,5},{5,1},{9,13},{13,9},{2,6},{6,2},{1... | collective-permute-start | bytes 196616 | tf_op jit(solution)/shard_map/ppermute | solution.py:186
  156.4 2.7 %collective-permute-start.28 = (bf16[64,512]{1,0:T(8,128)(2,1)S(1)}, bf16[64,512]{1,0:T(8,128)(2,1)S(1)}, u32[]{:S(2)}, u32[]{:S(2)}) collective-permute-start(bf16[64,512]{1,0:T(8,128)(2,1)S(1)} %activate.3.refs_0_), channel_id=1, source_target_pairs={{0,1},{1,0},{2,3},{3,2},{4,5},{5,4},{6,7},{7,6},{8,9},{9,8},{10,11... | collective-permute-start | bytes 196616 | tf_op jit(solution)/shard_map/ppermute | solution.py:186
  156.5 2.6 %collective-permute-start.30 = (bf16[64,512]{1,0:T(8,128)(2,1)S(1)}, bf16[64,512]{1,0:T(8,128)(2,1)S(1)}, u32[]{:S(2)}, u32[]{:S(2)}) collective-permute-start(bf16[64,512]{1,0:T(8,128)(2,1)S(1)} %collective-permute-done.26.refs_2_), channel_id=1, source_target_pairs={{0,1},{1,0},{2,3},{3,2},{4,5},{5,4},{6,7},{7,6},{8,9},{9,8},{10,11... | collective-permute-start | bytes 196616 | tf_op jit(solution)/shard_map/ppermute | solution.py:186
  157.0 2.1 %collective-permute-start.29 = (bf16[64,512]{1,0:T(8,128)(2,1)S(1)}, bf16[64,512]{1,0:T(8,128)(2,1)S(1)}, u32[]{:S(2)}, u32[]{:S(2)}) collective-permute-start(bf16[64,512]{1,0:T(8,128)(2,1)S(1)} %collective-permute-done.25.refs_1_), channel_id=1, source_target_pairs={{0,1},{1,0},{2,3},{3,2},{4,5},{5,4},{6,7},{7,6},{8,9},{9,8},{10,11... | collective-permute-start | bytes 196616 | tf_op jit(solution)/shard_map/ppermute | solution.py:186
  157.1 2.1 %collective-permute-start.31 = (bf16[64,512]{1,0:T(8,128)(2,1)S(1)}, bf16[64,512]{1,0:T(8,128)(2,1)S(1)}, u32[]{:S(2)}, u32[]{:S(2)}) collective-permute-start(bf16[64,512]{1,0:T(8,128)(2,1)S(1)} %collective-permute-done.27.refs_3_), channel_id=1, source_target_pairs={{0,1},{1,0},{2,3},{3,2},{4,5},{5,4},{6,7},{7,6},{8,9},{9,8},{10,11... | collective-permute-start | bytes 196616 | tf_op jit(solution)/shard_map/ppermute | solution.py:186
  160.5 5.5 %collective-permute-start.50 = (bf16[64,1024]{1,0:T(8,128)(2,1)S(1)}, bf16[64,1024]{1,0:T(8,128)(2,1)S(1)}, u32[]{:S(2)}, u32[]{:S(2)}) collective-permute-start(bf16[64,1024]{1,0:T(8,128)(2,1)S(1)} %get-tuple-element.90), channel_id=1, source_target_pairs={{0,2},{2,0},{1,3},{3,1},{4,6},{6,4},{5,7},{7,5},{8,10},{10,8},{9,1... | collective-permute-start | bytes 393224 | tf_op jit(solution)/shard_map/ppermute | solution.py:186
  (15 other events, 361.6 us)
